TPU v7x, 768 devices: a whole 4x8x12 slice. The times are simulated.
768 devices in a mesh: seq: 96 (over x, z, core), batch: 8 (over y).
Axes of the slice: x: 4, y: 8, z: 12, core: 2. Of those that a mesh axis runs over, the one named last changes fastest.
Arguments:
- queries: bfloat16 [8, 12288, 1024], P('batch', 'seq'), may hold values from -6 to 6
- keys: bfloat16 [8, 12288, 1024], P('batch', 'seq'), may hold values from -6 to 6
- values: bfloat16 [8, 12288, 1024], P('batch', 'seq'), may hold values from -6 to 6
- gates: bfloat16 [8, 12288, 1024], P('batch', 'seq'), may hold values from -6 to 6
- out_grad: bfloat16 [8, 12288, 1024], P('batch', 'seq'), may hold values from -6 to 6
- w_out: bfloat16 [1024, 1024], replicated, may hold values from -0.1875 to 0.1875
- hist_lengths: int32 [8, 4], P('batch'), may hold values from 1 to 8192, 12288 in all within a row
Outputs:
- output: bfloat16 [8, 12288, 1024], P('batch', 'seq')
- grad_queries: bfloat16 [8, 12288, 1024], P('batch', 'seq')
- grad_keys: bfloat16 [8, 12288, 1024], P('batch', 'seq')
- grad_values: bfloat16 [8, 12288, 1024], P('batch', 'seq')
- grad_gates: bfloat16 [8, 12288, 1024], P('batch', 'seq')
- grad_weight: float32 [1024, 1024], P('batch')
Inputs may be any that keep to these rules, and one draw needn't show every extreme that they name: `hist_lengths`: each group's 4 lengths sum to 12288, and the longest of each group is exactly 8192.
All inputs are finite; a program needn't handle non-finite values.
Results may differ from a plain program's by a relative error of at most 0.0058.
Values may be sent and summed in bfloat16 or wider, within the bound.
A program may use at most 64 MiB of HBM per device.

v0:
```python
import jax
import jax.numpy as jnp
from jax import lax
from jax.sharding import PartitionSpec as P

HEADS = 8
WINDOW = 256
REACH = 2


def shifted(block, axis, distance):
    devices = range(lax.axis_size(axis))
    route = [(i - distance, i) for i in devices if i - distance in devices]
    return lax.ppermute(block, axis, route)


def segment_start(positions, lengths):
    seg_ends = jnp.cumsum(lengths)
    seg_begins = seg_ends - lengths
    inside = (seg_begins[None, :] <= positions[:, None]) & (positions[:, None] < seg_ends[None, :])
    return jnp.sum(jnp.where(inside, seg_begins[None, :], 0), axis=1)


def silu_slope(scores):
    logistic = jax.nn.sigmoid(scores)
    return logistic * (1.0 + scores * (1.0 - logistic))


def causal_mask(query_pos, query_start, key_pos):
    inside = (key_pos[None, :] >= query_start[:, None]) & (key_pos[None, :] <= query_pos[:, None])
    return inside & (key_pos[None, :] > query_pos[:, None] - WINDOW)


def on_device(queries, keys, values, gates, out_grad, w_out, hist_lengths):
    query_rows = queries[0]
    key_rows = keys[0]
    value_rows = values[0]
    gate_rows = gates[0]
    grad_rows = out_grad[0]
    lengths = hist_lengths[0]
    row_total, model_width = query_rows.shape
    head_dim = model_width // HEADS
    score_scale = head_dim ** (-0.5)
    device = lax.axis_index("seq")
    local_iota = jnp.arange(row_total, dtype=jnp.int32)
    local_pos = device * row_total + local_iota
    local_start = segment_start(local_pos, lengths)
    stacked = jnp.stack((key_rows, value_rows))
    panels = [stacked]
    current = stacked
    for distance in range(REACH):
        current = shifted(current, "seq", 1)
        panels.append(current)
    window = jnp.concatenate(panels, axis=1)
    key_pos = jnp.concatenate(
        [(device - distance) * row_total + local_iota for distance in range(REACH + 1)]
    )
    key_heads = window[0].reshape(-1, HEADS, head_dim)
    value_heads = window[1].reshape(-1, HEADS, head_dim)
    query_heads = query_rows.reshape(row_total, HEADS, head_dim)
    scores = (
        jnp.einsum("ihe,jhe->hij", query_heads, key_heads, preferred_element_type=jnp.float32)
        * score_scale
    )
    allowed = causal_mask(local_pos, local_start, key_pos)[None]
    attention = jnp.where(allowed, jax.nn.silu(scores), 0.0).astype(jnp.bfloat16)
    mixed = jnp.einsum(
        "hij,jhe->ihe", attention, value_heads, preferred_element_type=jnp.float32
    ).reshape(row_total, model_width)
    centered = mixed - jnp.mean(mixed, axis=1, keepdims=True)
    inv_std = lax.rsqrt(jnp.mean(centered * centered, axis=1, keepdims=True) + 1e-05)
    normed = centered * inv_std
    hidden = (normed * gate_rows.astype(jnp.float32)).astype(jnp.bfloat16)
    output = jnp.dot(hidden, w_out, preferred_element_type=jnp.float32).astype(jnp.bfloat16)
    grad_hidden = lax.dot_general(
        grad_rows, w_out, (((1,), (1,)), ((), ())), preferred_element_type=jnp.float32
    )
    grad_gates = (grad_hidden * normed).astype(jnp.bfloat16)
    grad_norm = grad_hidden * gate_rows.astype(jnp.float32)
    grad_mix = (
        (
            grad_norm
            - jnp.mean(grad_norm, axis=1, keepdims=True)
            - normed * jnp.mean(grad_norm * normed, axis=1, keepdims=True)
        )
        * inv_std
    ).astype(jnp.bfloat16)
    mix_heads = grad_mix.reshape(row_total, HEADS, head_dim)
    grad_attention = jnp.einsum(
        "ihe,jhe->hij", mix_heads, value_heads, preferred_element_type=jnp.float32
    )
    grad_scores = jnp.where(allowed, grad_attention * silu_slope(scores) * score_scale, 0.0).astype(
        jnp.bfloat16
    )
    grad_queries = (
        jnp.einsum("hij,jhe->ihe", grad_scores, key_heads, preferred_element_type=jnp.float32)
        .reshape(row_total, model_width)
        .astype(jnp.bfloat16)
    )
    grad_key_all = jnp.einsum(
        "hij,ihe->jhe", grad_scores, query_heads, preferred_element_type=jnp.float32
    ).reshape(-1, model_width)
    grad_value_all = jnp.einsum(
        "hij,ihe->jhe", attention, mix_heads, preferred_element_type=jnp.float32
    ).reshape(-1, model_width)
    totals = jnp.stack((grad_key_all[:row_total], grad_value_all[:row_total]))
    for distance in range(1, REACH + 1):
        partial_grads = jnp.stack(
            (
                grad_key_all[distance * row_total : (distance + 1) * row_total],
                grad_value_all[distance * row_total : (distance + 1) * row_total],
            )
        )
        totals = totals + shifted(partial_grads, "seq", -distance)
    grad_keys = totals[0].astype(jnp.bfloat16)
    grad_values = totals[1].astype(jnp.bfloat16)
    weight_share = lax.psum_scatter(
        lax.dot_general(
            hidden, grad_rows, (((0,), (0,)), ((), ())), preferred_element_type=jnp.float32
        ),
        "batch",
        scatter_dimension=0,
        tiled=True,
    )
    token_total = row_total * lax.axis_size("seq") * lax.axis_size("batch")
    grad_weight = lax.psum(weight_share, "seq") * token_total ** (-0.5)
    return (
        output[None],
        grad_queries[None],
        grad_keys[None],
        grad_values[None],
        grad_gates[None],
        grad_weight,
    )


def solution(mesh):
    placed = (
        P("batch", "seq", None),
        P("batch", "seq", None),
        P("batch", "seq", None),
        P("batch", "seq", None),
        P("batch", "seq", None),
        P(),
        P("batch", None),
    )
    return jax.shard_map(
        on_device,
        mesh=mesh,
        in_specs=placed,
        out_specs=(
            P("batch", "seq", None),
            P("batch", "seq", None),
            P("batch", "seq", None),
            P("batch", "seq", None),
            P("batch", "seq", None),
            P("batch", None),
        ),
        check_vma=False,
    )
```

profile of v0, /device:TPU:1, one launch (start us, length us, event | category | flops | bytes accessed | tf_op | source)
XLA Modules:
  0.0 391.4 jit_solution(12225941627831172617)
XLA Ops:
  7.2 1.3 copy.56
  10.5 5.4 %collective-permute-start = (bf16[2,128,1024]{1,2,0:T(8,128)(2,1)}, bf16[2,128,1024]{1,2,0:T(8,128)(2,1)}, u32[]{:S(2)}, u32[]{:S(2)}) collective-permute-start(bf16[2,128,1024]{1,2,0:T(8,128)(2,1)} %pad_maximum_fusion.3), channel_id=1, source_target_pairs={{0,8},{8,16},{16,24},{24,32},{32,40},{40,48},{48,56},{56,64},{64,7... | collective-permute-start | bytes 1572872 | tf_op jit(solution)/shard_map/ppermute | solution.py:14
  17.3 6.8 %collective-permute-done = bf16[2,128,1024]{1,2,0:T(8,128)(2,1)} collective-permute-done((bf16[2,128,1024]{1,2,0:T(8,128)(2,1)}, bf16[2,128,1024]{1,2,0:T(8,128)(2,1)}, u32[]{:S(2)}, u32[]{:S(2)}) %collective-permute-start) | collective-permute-done | bytes 524320 | tf_op jit(solution)/shard_map/ppermute | solution.py:14
  24.0 2.7 collective-permute-start.1
  26.9 6.2 %collective-permute-done.1 = bf16[2,128,1024]{1,2,0:T(8,128)(2,1)S(1)} collective-permute-done((bf16[2,128,1024]{1,2,0:T(8,128)(2,1)}, bf16[2,128,1024]{1,2,0:T(8,128)(2,1)S(1)}, u32[]{:S(2)}, u32[]{:S(2)}) %collective-permute-start.1) | collective-permute-done | bytes 524320 | tf_op jit(solution)/shard_map/ppermute | solution.py:14
  33.1 1.3 pad_maximum_fusion
  34.6 2.0 fusion.4
  38.0 2.6 fusion.17
  40.9 1.9 fusion.24
  44.0 2.7 fusion.10
  47.2 1.2 fusion.26
  48.4 1.2 copy.74
  49.7 2.1 copy.72
  51.7 1.7 convolution_bitcast_fusion
  54.6 2.0 copy.75
  56.6 2.0 copy.73
  58.7 2.3 pad_maximum_fusion.1
  61.0 2.0 collective-permute-start.2
  64.2 1.3 collective-permute-start.3
  68.0 2.1 copy.71
  71.2 37.6 %reduce-scatter.2.cloned.1.call-done = f32[128,1024]{1,0:T(8,128)} async-done(((f32[1024,1024]{1,0:T(8,128)}), f32[128,1024]{1,0:T(8,128)}) %reduce-scatter.2.cloned.1.call-update) | async-done | bytes 524304 | tf_op jit(solution)/shard_map/reduce_scatter | solution.py:117
  108.9 1.9 fusion.13
  111.6 271.1 %all-reduce.2.cloned.1.call-done = f32[128,1024]{1,0:T(8,128)} async-done(((f32[128,1024]{1,0:T(8,128)}), f32[128,1024]{1,0:T(8,128)}) %all-reduce.2.cloned.1.call-update) | async-done | bytes 524304 | tf_op jit(solution)/shard_map/psum | solution.py:126
  382.7 1.9 broadcast_multiply_fusion
  (68 shorter events, 13.8 us)
Async XLA Ops:
  7.2 33.7 %copy-start = (bf16[1024,1024]{1,0:T(8,128)(2,1)S(1)}, bf16[1024,1024]{1,0:T(8,128)(2,1)}, u32[]{:S(2)}) copy-start(bf16[1024,1024]{1,0:T(8,128)(2,1)} %param.12) | copy-start | bytes 6291460
  7.2 8.7 %copy-start.14 = (bf16[1,128,1024]{2,1,0:T(8,128)(2,1)S(1)}, bf16[1,128,1024]{2,1,0:T(8,128)(2,1)}, u32[]{:S(2)}) copy-start(bf16[1,128,1024]{2,1,0:T(8,128)(2,1)} %param.7) | copy-start | bytes 786436
  7.2 8.9 %copy-start.1 = (bf16[1,128,1024]{2,1,0:T(8,128)(2,1)S(1)}, bf16[1,128,1024]{2,1,0:T(8,128)(2,1)}, u32[]{:S(2)}) copy-start(bf16[1,128,1024]{2,1,0:T(8,128)(2,1)} %param.10) | copy-start | bytes 786436
  7.2 101.7 %reduce-scatter.2.cloned.1.call-start = ((), (), s32[]{:S(2)}) async-start(), calls=%async_computation.1 | async-start | bytes 4718592 | tf_op jit(solution)/shard_map/reduce_scatter | solution.py:117
  8.5 8.5 %copy-start.15 = (s32[1,4]{1,0:T(1,128)S(1)}, s32[1,4]{1,0:T(1,128)}, u32[]{:S(2)}) copy-start(s32[1,4]{1,0:T(1,128)} %param.13) | copy-start | bytes 52
  10.5 13.5 %collective-permute-start = (bf16[2,128,1024]{1,2,0:T(8,128)(2,1)}, bf16[2,128,1024]{1,2,0:T(8,128)(2,1)}, u32[]{:S(2)}, u32[]{:S(2)}) collective-permute-start(bf16[2,128,1024]{1,2,0:T(8,128)(2,1)} %pad_maximum_fusion.3), channel_id=1, source_target_pairs={{0,8},{8,16},{16,24},{24,32},{32,40},{40,48},{48,56},{56,64},{64,7... | collective-permute-start | bytes 1572872 | tf_op jit(solution)/shard_map/ppermute | solution.py:14
  16.1 18.5 %copy-start.11 = (bf16[1,128,1024]{1,2,0:T(8,128)(2,1)}, bf16[1,128,1024]{1,2,0:T(8,128)(2,1)S(1)}, u32[]{:S(2)}) copy-start(bf16[1,128,1024]{1,2,0:T(8,128)(2,1)S(1)} %copy.85) | copy-start | bytes 786436
  24.0 9.1 %collective-permute-start.1 = (bf16[2,128,1024]{1,2,0:T(8,128)(2,1)}, bf16[2,128,1024]{1,2,0:T(8,128)(2,1)S(1)}, u32[]{:S(2)}, u32[]{:S(2)}) collective-permute-start(bf16[2,128,1024]{1,2,0:T(8,128)(2,1)} %collective-permute-done), channel_id=1, source_target_pairs={{0,8},{8,16},{16,24},{24,32},{32,40},{40,48},{48,56},{56,64},{64,7... | collective-permute-start | bytes 1572872 | tf_op jit(solution)/shard_map/ppermute | solution.py:14
  34.6 2.0 copy-start.2
  34.6 2.0 copy-start.7
  36.6 1.4 copy-start.6
  36.6 1.3 copy-start.8
  36.6 1.4 copy-start.10
  40.7 342.0 %all-reduce.2.cloned.1.call-start = ((), (), s32[]{:S(2)}) async-start(), calls=%async_computation.2 | async-start | bytes 1048576 | tf_op jit(solution)/shard_map/psum | solution.py:126
  44.0 2.7 copy-start.13
  44.0 2.7 copy-start.12
  46.7 1.7 copy-start.4
  58.7 4.4 %copy-start.9 = (f32[1,128,1024]{2,1,0:T(8,128)S(1)}, f32[1,128,1024]{2,1,0:T(8,128)}, u32[]{:S(2)}) copy-start(f32[1,128,1024]{2,1,0:T(8,128)} %copy.75) | copy-start | bytes 1572868
  61.0 4.5 %copy-start.3 = (bf16[1,384,1024]{1,2,0:T(8,128)(2,1)S(1)}, bf16[1,384,1024]{1,2,0:T(8,128)(2,1)}, u32[]{:S(2)}) copy-start(bf16[1,384,1024]{1,2,0:T(8,128)(2,1)} %copy-done.2) | copy-start | bytes 2359300
  61.0 4.5 %copy-start.5 = (bf16[8,128,384]{1,2,0:T(8,128)(2,1)S(1)}, bf16[8,128,384]{1,2,0:T(8,128)(2,1)}, u32[]{:S(2)}) copy-start(bf16[8,128,384]{1,2,0:T(8,128)(2,1)} %copy-done.4) | copy-start | bytes 2359300
  61.0 47.9 %collective-permute-start.2 = (f32[2,128,1024]{2,1,0:T(8,128)}, f32[2,128,1024]{2,1,0:T(8,128)}, u32[]{:S(2)}, u32[]{:S(2)}) collective-permute-start(f32[2,128,1024]{2,1,0:T(8,128)} %pad_maximum_fusion.1), channel_id=1, source_target_pairs={{8,0},{16,8},{24,16},{32,24},{40,32},{48,40},{56,48},{64,56},{72,6... | collective-permute-start | bytes 3145736 | tf_op jit(solution)/shard_map/ppermute | solution.py:14
  64.2 44.7 %collective-permute-start.3 = (f32[2,128,1024]{2,1,0:T(8,128)}, f32[2,128,1024]{2,1,0:T(8,128)}, u32[]{:S(2)}, u32[]{:S(2)}) collective-permute-start(f32[2,128,1024]{2,1,0:T(8,128)} %pad_maximum_fusion.2), channel_id=1, source_target_pairs={{16,0},{24,8},{32,16},{40,24},{48,32},{56,40},{64,48},{72,56},{80,... | collective-permute-start | bytes 3145736 | tf_op jit(solution)/shard_map/ppermute | solution.py:14
Sparse Core Ops, SparseCore 0:
  40.8 68.0 reduce-scatter.1
  112.4 270.2 all-reduce.1
where the time goes:
time: 392 us; the launch traced here: 391 us
  waiting for transfers between devices  322 us (82%)
  local copies, waits for them, and re-layouts  19.6 us (5%)
  between operations  14.4 us (4%)
  matrix products  13.3 us (3%)
  starting transfers between devices  11.4 us (3%)
  other arithmetic  10.9 us (3%)
    psum x1, waiting for transfers between devices, on_device(): grad_weight = lax.psum(weight_share, 'seq') * token_total ** (-0.5)  271 us
    reduce_scatter x1, waiting for transfers between devices, on_device(): lax.psum_scatter(lax.dot_general(hidden, grad_rows, (((0,), (0,)), ((), (...  37.6 us
    ppermute x4, waiting for transfers between devices, shifted(): return lax.ppermute(block, axis, route)  13 us
    ppermute x4, starting transfers between devices, shifted(): return lax.ppermute(block, axis, route)  11.4 us
  transfers between devices with their start and end apart: 6, of which 4 were waited for; matrix products, arithmetic and copies ran while one was open for 8% of the time, Pallas kernels for 0%

commit v1 on v0

--- a/solution.py
+++ b/solution.py
@@ -1,11 +1,17 @@
+import functools
+
 import jax
 import jax.numpy as jnp
 from jax import lax
+from jax.experimental import pallas as pl
+from jax.experimental.pallas import tpu as pltpu
 from jax.sharding import PartitionSpec as P
 
 HEADS = 8
 WINDOW = 256
 REACH = 2
+NX, NY, NZ = 4, 8, 12
+MESH = pl.DeviceIdType.MESH
 
 
 def shifted(block, axis, distance):
@@ -29,6 +35,118 @@
 def causal_mask(query_pos, query_start, key_pos):
     inside = (key_pos[None, :] >= query_start[:, None]) & (key_pos[None, :] <= query_pos[:, None])
     return inside & (key_pos[None, :] > query_pos[:, None] - WINDOW)
+
+
+def reduce_kernel(scale, g_ref, out_ref, sc, rc, s0, rx, s1, ry, s2, rz, ag, fin, send_sem, rc_sem, rx_sem, ry_sem, rz_sem, ag_sem, fin_sem):
+    f32, bf16 = jnp.float32, jnp.bfloat16
+    seq = lax.axis_index("seq")
+    y = lax.axis_index("batch")
+    k = lax.rem(seq, 2)
+    x = seq // (2 * NZ)
+    z = lax.rem(seq // 2, NZ)
+
+    def dev(px, py, pz, pk):
+        return {"seq": (px * NZ + pz) * 2 + pk, "batch": py}
+
+    partner = dev(x, y, z, 1 - k)
+    xs = [dev(lax.rem(x + d, NX), y, z, k) for d in range(1, NX)]
+    xo = [dev(lax.rem(x + d, NX), y, z, 1 - k) for d in range(1, NX)]
+    ys = [dev(x, lax.rem(y + d, NY), z, k) for d in range(1, NY)]
+    zs = [dev(x, y, lax.rem(z + d, NZ), k) for d in range(1, NZ)]
+    barrier = pltpu.get_barrier_semaphore()
+    everyone = [partner] + xs + xo + ys + zs
+    for peer in everyone:
+        pl.semaphore_signal(barrier, inc=1, device_id=peer, device_id_type=MESH)
+
+    sends = []
+
+    def send(src, dst, recv_sem, peer):
+        copy = pltpu.make_async_remote_copy(
+            src_ref=src, dst_ref=dst, send_sem=send_sem.at[len(sends)], recv_sem=recv_sem,
+            device_id=peer, device_id_type=MESH)
+        copy.start()
+        sends.append(copy)
+        return copy
+
+    other = pl.multiple_of((1 - k) * 512, 512)
+    own = pl.multiple_of(k * 512, 512)
+    sc[...] = g_ref[:, pl.ds(other, 512)].astype(bf16)
+    pl.semaphore_wait(barrier, len(everyone))
+
+    c = send(sc, rc, rc_sem, partner)
+    c.wait_recv()
+    for j in range(NX):
+        for i in range(NY):
+            rows = pl.ds(i * 128 + j * 32, 32)
+            s0[j, i] = (g_ref[rows, pl.ds(own, 512)] + rc[rows, :].astype(f32)).astype(bf16)
+
+    cs = [send(s0.at[lax.rem(x + d, NX)], rx.at[d - 1], rx_sem.at[d - 1], xs[d - 1]) for d in range(1, NX)]
+    for c in cs:
+        c.wait_recv()
+    for i in range(NY):
+        t = s0[x, i].astype(f32)
+        for d in range(NX - 1):
+            t = t + rx[d, i].astype(f32)
+        s1[i] = t.astype(bf16)
+
+    cs = [send(s1.at[lax.rem(y + d, NY)], ry.at[d - 1], ry_sem.at[d - 1], ys[d - 1]) for d in range(1, NY)]
+    for c in cs:
+        c.wait_recv()
+    t = s1[y].astype(f32)
+    for d in range(NY - 1):
+        t = t + ry[d].astype(f32)
+    for r in range(2):
+        for j in range(4):
+            s2[r * 4 + j] = t[r * 16:r * 16 + 16, j * 128:j * 128 + 128].astype(bf16)
+    s2[8:] = jnp.zeros((NZ - 8, 16, 128), bf16)
+
+    cs = [send(s2.at[lax.rem(z + d, NZ)], rz.at[d - 1], rz_sem.at[d - 1], zs[d - 1]) for d in range(1, NZ)]
+    for c in cs:
+        c.wait_recv()
+    t = s2[z].astype(f32)
+    for d in range(NZ - 1):
+        t = t + rz[d].astype(f32)
+    ag[z] = t.astype(bf16)
+    cs = [send(ag.at[z], ag.at[z], ag_sem.at[d - 1], zs[d - 1]) for d in range(1, NZ)]
+    for c in cs:
+        c.wait_recv()
+
+    slot = x * 2 + k
+    fin[slot] = ag[0:8]
+    peers = [partner] + xs + xo
+    cs = [send(ag.at[pl.ds(0, 8)], fin.at[slot], fin_sem.at[i], p) for i, p in enumerate(peers)]
+    for c in cs:
+        c.wait_recv()
+    for px in range(NX):
+        for pk in range(2):
+            for r in range(2):
+                for j in range(4):
+                    out_ref[px * 32 + r * 16:px * 32 + r * 16 + 16, pk * 512 + j * 128:pk * 512 + j * 128 + 128] = (
+                        fin[px * 2 + pk, r * 4 + j].astype(f32) * scale)
+    for c in sends:
+        c.wait_send()
+
+
+def reduce_weight(g, scale):
+    bf16 = jnp.bfloat16
+    vm = pltpu.VMEM
+    dma = pltpu.SemaphoreType.DMA
+    n_sends = 1 + (NX - 1) + (NY - 1) + 2 * (NZ - 1) + 7
+    return pl.pallas_call(
+        functools.partial(reduce_kernel, scale),
+        out_shape=jax.ShapeDtypeStruct((128, 1024), jnp.float32),
+        in_specs=[pl.BlockSpec(memory_space=pltpu.VMEM)],
+        out_specs=pl.BlockSpec(memory_space=pltpu.VMEM),
+        scratch_shapes=[
+            vm((1024, 512), bf16), vm((1024, 512), bf16),
+            vm((NX, NY, 32, 512), bf16), vm((NX - 1, NY, 32, 512), bf16),
+            vm((NY, 32, 512), bf16), vm((NY - 1, 32, 512), bf16),
+            vm((NZ, 16, 128), bf16), vm((NZ - 1, 16, 128), bf16),
+            vm((NZ, 16, 128), bf16), vm((8, 8, 16, 128), bf16),
+            dma((n_sends,)), dma, dma((NX - 1,)), dma((NY - 1,)), dma((NZ - 1,)), dma((NZ - 1,)), dma((7,)),
+        ],
+        compiler_params=pltpu.CompilerParams(collective_id=0, has_side_effects=True, vmem_limit_bytes=40 << 20),
+    )(g)
 
 
 def on_device(queries, keys, values, gates, out_grad, w_out, hist_lengths):
@@ -114,16 +232,13 @@
         totals = totals + shifted(partial_grads, "seq", -distance)
     grad_keys = totals[0].astype(jnp.bfloat16)
     grad_values = totals[1].astype(jnp.bfloat16)
-    weight_share = lax.psum_scatter(
+    token_total = row_total * lax.axis_size("seq") * lax.axis_size("batch")
+    grad_weight = reduce_weight(
         lax.dot_general(
             hidden, grad_rows, (((0,), (0,)), ((), ())), preferred_element_type=jnp.float32
         ),
-        "batch",
-        scatter_dimension=0,
-        tiled=True,
-    )
-    token_total = row_total * lax.axis_size("seq") * lax.axis_size("batch")
-    grad_weight = lax.psum(weight_share, "seq") * token_total ** (-0.5)
+        token_total ** (-0.5),
+    )
     return (
         output[None],
         grad_queries[None],

time: 392 us -> 154 us (0.39)
  waiting for transfers between devices: 322 us -> 13 us
  Pallas kernels: 0 us -> 80 us
  between operations: 14.4 us -> 0.97 us
  local copies, waits for them, and re-layouts: 19.6 us -> 25.5 us
    psum x1 -> x0, waiting for transfers between devices: 271 us -> none  [on_device(): grad_weight = lax.psum(weight_share, 'seq') * token_total ** (-0.5)]
    pallas_call x0 -> x1, Pallas kernels: none -> 80 us  [reduce_weight(): pl.pallas_call(functools.partial(reduce_kernel, scale), out_shape=jax.Sha...]
    reduce_scatter x1 -> x0, waiting for transfers between devices: 37.6 us -> none  [on_device(): lax.psum_scatter(lax.dot_general(hidden, grad_rows, (((0,), (0,)), ((), (...]
  transfers between devices with their start and end apart: 6 -> 4, of which waited for: 4 -> 2; matrix products, arithmetic and copies ran while one was open for 8% -> 9% of each run, Pallas kernels for 0% -> 52%
where the time goes in v1:
time: 154 us; the launch traced here: 153 us
  Pallas kernels  80 us (52%)
  local copies, waits for them, and re-layouts  25.5 us (17%)
  waiting for transfers between devices  13 us (8%)
  matrix products  12.5 us (8%)
  starting transfers between devices  11.4 us (7%)
  other arithmetic  10.1 us (7%)
    pallas_call x1, Pallas kernels, reduce_weight(): pl.pallas_call(functools.partial(reduce_kernel, scale), out_shape=jax.Sha...  80 us
    ppermute x4, waiting for transfers between devices, shifted(): return lax.ppermute(block, axis, route)  13 us
    ppermute x4, starting transfers between devices, shifted(): return lax.ppermute(block, axis, route)  11.4 us
    another operation x4, local copies, waits for them, and re-layouts, on_device(): jnp.stack((grad_key_all[distance * row_total:(distance + 1) * row_total],...  8.19 us
    unnamed x42, local copies, waits for them, and re-layouts  5.42 us
    another operation x2, local copies, waits for them, and re-layouts, on_device(): totals = jnp.stack((grad_key_all[:row_total], grad_value_all[:row_total]))  4.08 us
    slice x2, local copies, waits for them, and re-layouts, on_device(): totals = jnp.stack((grad_key_all[:row_total], grad_value_all[:row_total]))  3.77 us
    another operation x2, other arithmetic, on_device(): jnp.stack((grad_key_all[distance * row_total:(distance + 1) * row_total],...  3.51 us
  transfers between devices with their start and end apart: 4, of which 2 were waited for; matrix products, arithmetic and copies ran while one was open for 9% of the time, Pallas kernels for 52%

profile of v1, /device:TPU:1, one launch (start us, length us, event | category | flops | bytes accessed | tf_op | source)
XLA Modules:
  0.0 153.5 jit_solution(557046120123222593)
XLA Ops:
  0.7 1.3 copy.56
  3.9 5.4 %collective-permute-start = (bf16[2,128,1024]{1,2,0:T(8,128)(2,1)}, bf16[2,128,1024]{1,2,0:T(8,128)(2,1)}, u32[]{:S(2)}, u32[]{:S(2)}) collective-permute-start(bf16[2,128,1024]{1,2,0:T(8,128)(2,1)} %pad_maximum_fusion.3), channel_id=1, source_target_pairs={{0,8},{8,16},{16,24},{24,32},{32,40},{40,48},{48,56},{56,64},{64,7... | collective-permute-start | bytes 1572872 | tf_op jit(solution)/shard_map/ppermute | solution.py:20
  10.7 6.8 %collective-permute-done = bf16[2,128,1024]{1,2,0:T(8,128)(2,1)} collective-permute-done((bf16[2,128,1024]{1,2,0:T(8,128)(2,1)}, bf16[2,128,1024]{1,2,0:T(8,128)(2,1)}, u32[]{:S(2)}, u32[]{:S(2)}) %collective-permute-start) | collective-permute-done | bytes 524320 | tf_op jit(solution)/shard_map/ppermute | solution.py:20
  17.5 2.7 %collective-permute-start.1 = (bf16[2,128,1024]{1,2,0:T(8,128)(2,1)}, bf16[2,128,1024]{1,2,0:T(8,128)(2,1)S(1)}, u32[]{:S(2)}, u32[]{:S(2)}) collective-permute-start(bf16[2,128,1024]{1,2,0:T(8,128)(2,1)} %collective-permute-done), channel_id=1, source_target_pairs={{0,8},{8,16},{16,24},{24,32},{32,40},{40,48},{48,56},{56,64},{64,7... | collective-permute-start | bytes 1572872 | tf_op jit(solution)/shard_map/ppermute | solution.py:20
  20.4 6.2 %collective-permute-done.1 = bf16[2,128,1024]{1,2,0:T(8,128)(2,1)S(1)} collective-permute-done((bf16[2,128,1024]{1,2,0:T(8,128)(2,1)}, bf16[2,128,1024]{1,2,0:T(8,128)(2,1)S(1)}, u32[]{:S(2)}, u32[]{:S(2)}) %collective-permute-start.1) | collective-permute-done | bytes 524320 | tf_op jit(solution)/shard_map/ppermute | solution.py:20
  26.5 1.3 pad_maximum_fusion
  28.0 1.9 %fusion.4 = (bf16[8,128,384]{1,2,0:T(8,128)(2,1)S(1)}, f32[8,384,128]{2,1,0:T(8,128)}) fusion(pred[128,384]{0,1:T(8,128)(4,1)S(1)} %compare_and_fusion, bf16[384,8,128]{0,2,1:T(8,128)(2,1)S(1)} %bitcast.104, bf16[128,8,128]{0,2,1:T(8,128)(2,1)S(1)} %bitcast.115), kind=kOutput, calls=%fused_computation.8 | convolution fusion | flops 103415808 | bytes 3457024 | tf_op jit(solution)/shard_map/ihe,jhe->hij/dot_general | solution.py:180
  31.1 1.9 %fusion.24 = (f32[128]{0:T(128)S(1)}, f32[128]{0:T(128)S(1)}, f32[128,1024]{1,0:T(8,128)S(1)}) fusion(bf16[1,128,1024]{2,1,0:T(8,128)(2,1)S(1)} %copy-done.1, f32[128]{0:T(128)S(1)} %add_rsqrt_fusion, f32[128,1024]{1,0:T(8,128)S(1)} %copy.61, f32[128]{0:T(128)S(1)} %broadcast_multiply_fusion.2, bf16[1024,1024]{1,0:T(8,128)(2,1)S(1)} %copy-done, ...), kind=kOutput, calls=%fused_computation.45 | convolution fusion | flops 269352704 | bytes 3672064 | tf_op jit(solution)/shard_map/dot_general | solution.py:193
  34.0 1.8 %copy.86 = bf16[128,1024]{0,1:T(8,128)(2,1)} copy(bf16[128,1024]{1,0:T(8,128)(2,1)} %get-tuple-element.35) | data formatting | bytes 524288 | tf_op jit(solution)/shard_map/reshape | solution.py:206
  35.8 3.0 %convolution_bitcast_fusion = f32[384,8,128]{0,2,1:T(8,128)} fusion(bf16[128,8,128]{0,2,1:T(8,128)(2,1)} %bitcast.117, bf16[8,128,384]{1,2,0:T(8,128)(2,1)} %copy-done.8), kind=kOutput, calls=%fused_computation.15 | convolution fusion | flops 100663296 | bytes 2621440 | tf_op jit(solution)/shard_map/hij,ihe->jhe/dot_general | solution.py:221
  41.4 2.0 %copy.74 = f32[1,128,1024]{2,1,0:T(8,128)} copy(f32[1,128,1024]{1,2,0:T(8,128)} %bitcast.113) | data formatting | bytes 1048576 | tf_op jit(solution)/shard_map/stack | solution.py:226
  43.5 2.1 %copy.72 = f32[1,128,1024]{2,1,0:T(8,128)} copy(f32[1,128,1024]{1,2,0:T(8,128)} %bitcast.111) | data formatting | bytes 1048576 | tf_op jit(solution)/shard_map/stack | solution.py:226
  45.5 2.6 %fusion.27 = (f32[128,8,128]{0,2,1:T(8,128)}, f32[128,8,128]{0,2,1:T(8,128)}, f32[128,8,128]{0,2,1:T(8,128)}) fusion(f32[384,8,128]{0,2,1:T(8,128)} %convolution_bitcast_fusion), kind=kLoop, calls=%fused_computation.60 | loop fusion | bytes 3145728 | tf_op jit(solution)/shard_map/slice | solution.py:224
  48.1 2.0 %copy.75 = f32[1,128,1024]{2,1,0:T(8,128)} copy(f32[1,128,1024]{1,2,0:T(8,128)} %bitcast.114) | data formatting | bytes 1048576 | tf_op jit(solution)/shard_map/stack | solution.py:226
  50.2 2.0 %copy.73 = f32[1,128,1024]{2,1,0:T(8,128)} copy(f32[1,128,1024]{1,2,0:T(8,128)} %bitcast.112) | data formatting | bytes 1048576 | tf_op jit(solution)/shard_map/stack | solution.py:226
  52.2 2.4 %pad_maximum_fusion.1 = f32[2,128,1024]{2,1,0:T(8,128)} fusion(f32[1,128,1024]{2,1,0:T(8,128)} %copy.73, f32[1,128,1024]{2,1,0:T(8,128)} %copy.72), kind=kLoop, calls=%fused_computation.24 | loop fusion | flops 262144 | bytes 2097152 | tf_op jit(solution)/shard_map/stack | solution.py:226
  54.6 2.0 %collective-permute-start.2 = (f32[2,128,1024]{2,1,0:T(8,128)}, f32[2,128,1024]{2,1,0:T(8,128)}, u32[]{:S(2)}, u32[]{:S(2)}) collective-permute-start(f32[2,128,1024]{2,1,0:T(8,128)} %pad_maximum_fusion.1), channel_id=1, source_target_pairs={{8,0},{16,8},{24,16},{32,24},{40,32},{48,40},{56,48},{64,56},{72,6... | collective-permute-start | bytes 3145736 | tf_op jit(solution)/shard_map/ppermute | solution.py:20
  57.8 1.3 collective-permute-start.3
  60.2 1.8 %copy.77 = bf16[1,128,1024]{2,1,0:T(8,128)(2,1)} copy(bf16[1,128,1024]{1,2,0:T(8,128)(2,1)} %bitcast.119) | data formatting | bytes 524288
  62.0 2.0 %copy.70 = f32[1,128,1024]{2,1,0:T(8,128)} copy(f32[1,128,1024]{1,2,0:T(8,128)} %bitcast.109) | data formatting | bytes 1048576 | tf_op jit(solution)/shard_map/stack | solution.py:224
  64.0 2.0 %copy.71 = f32[1,128,1024]{2,1,0:T(8,128)} copy(f32[1,128,1024]{1,2,0:T(8,128)} %bitcast.110) | data formatting | bytes 1048576 | tf_op jit(solution)/shard_map/stack | solution.py:224
  67.2 1.6 %fusion.17.g_ref = f32[1024,1024]{1,0:T(8,128)S(1)} fusion(bf16[128,1024]{0,1:T(8,128)(2,1)S(1)} %bitcast.120, bf16[1,128,1024]{2,1,0:T(8,128)(2,1)} %param.11), kind=kOutput, calls=%fused_computation.38 | convolution fusion | flops 268435456 | bytes 4718592 | tf_op jit(solution)/shard_map/dot_general | solution.py:237
  68.8 80.0 %shard_map.118 = f32[128,1024]{1,0:T(8,128)S(1)} custom-call(f32[1024,1024]{1,0:T(8,128)S(1)} %fusion.17.g_ref), custom_call_target="tpu_custom_call" | custom-call | tf_op jit(solution)/shard_map/pallas_call | solution.py:135
  150.1 1.8 %fusion.13 = bf16[2,128,1024]{2,1,0:T(8,128)(2,1)S(1)} fusion(f32[2,128,1024]{2,1,0:T(8,128)} %collective-permute-done.3, f32[2,128,1024]{2,1,0:T(8,128)} %collective-permute-done.2, f32[1,128,1024]{2,1,0:T(8,128)S(1)} %copy-done.10, f32[1,128,1024]{2,1,0:T(8,128)S(1)} %copy-done.9), kind=kLoop, calls=%fused_computation.23 | loop fusion | flops 1048576 | bytes 3670016 | tf_op jit(solution)/shard_map/convert.3
  (69 shorter events, 14.6 us)
Async XLA Ops:
  0.6 30.4 %copy-start = (bf16[1024,1024]{1,0:T(8,128)(2,1)S(1)}, bf16[1024,1024]{1,0:T(8,128)(2,1)}, u32[]{:S(2)}) copy-start(bf16[1024,1024]{1,0:T(8,128)(2,1)} %param.12) | copy-start | bytes 6291460
  0.6 8.7 %copy-start.16 = (bf16[1,128,1024]{2,1,0:T(8,128)(2,1)S(1)}, bf16[1,128,1024]{2,1,0:T(8,128)(2,1)}, u32[]{:S(2)}) copy-start(bf16[1,128,1024]{2,1,0:T(8,128)(2,1)} %param.7) | copy-start | bytes 786436
  0.7 8.9 %copy-start.1 = (bf16[1,128,1024]{2,1,0:T(8,128)(2,1)S(1)}, bf16[1,128,1024]{2,1,0:T(8,128)(2,1)}, u32[]{:S(2)}) copy-start(bf16[1,128,1024]{2,1,0:T(8,128)(2,1)} %param.10) | copy-start | bytes 786436
  1.9 8.5 %copy-start.17 = (s32[1,4]{1,0:T(1,128)S(1)}, s32[1,4]{1,0:T(1,128)}, u32[]{:S(2)}) copy-start(s32[1,4]{1,0:T(1,128)} %param.13) | copy-start | bytes 52
  3.9 13.5 %collective-permute-start = (bf16[2,128,1024]{1,2,0:T(8,128)(2,1)}, bf16[2,128,1024]{1,2,0:T(8,128)(2,1)}, u32[]{:S(2)}, u32[]{:S(2)}) collective-permute-start(bf16[2,128,1024]{1,2,0:T(8,128)(2,1)} %pad_maximum_fusion.3), channel_id=1, source_target_pairs={{0,8},{8,16},{16,24},{24,32},{32,40},{40,48},{48,56},{56,64},{64,7... | collective-permute-start | bytes 1572872 | tf_op jit(solution)/shard_map/ppermute | solution.py:20
  9.5 18.5 %copy-start.13 = (bf16[1,128,1024]{1,2,0:T(8,128)(2,1)}, bf16[1,128,1024]{1,2,0:T(8,128)(2,1)S(1)}, u32[]{:S(2)}) copy-start(bf16[1,128,1024]{1,2,0:T(8,128)(2,1)S(1)} %copy.85) | copy-start | bytes 786436
  17.5 9.1 %collective-permute-start.1 = (bf16[2,128,1024]{1,2,0:T(8,128)(2,1)}, bf16[2,128,1024]{1,2,0:T(8,128)(2,1)S(1)}, u32[]{:S(2)}, u32[]{:S(2)}) collective-permute-start(bf16[2,128,1024]{1,2,0:T(8,128)(2,1)} %collective-permute-done), channel_id=1, source_target_pairs={{0,8},{8,16},{16,24},{24,32},{32,40},{40,48},{48,56},{56,64},{64,7... | collective-permute-start | bytes 1572872 | tf_op jit(solution)/shard_map/ppermute | solution.py:20
  28.0 2.0 %copy-start.2 = (bf16[1,384,1024]{1,2,0:T(8,128)(2,1)}, bf16[1,384,1024]{1,2,0:T(8,128)(2,1)S(1)}, u32[]{:S(2)}) copy-start(bf16[1,384,1024]{1,2,0:T(8,128)(2,1)S(1)} %get-tuple-element.32) | copy-start | bytes 2359300
  28.0 2.0 %copy-start.6 = (bf16[1,384,1024]{1,2,0:T(8,128)(2,1)}, bf16[1,384,1024]{1,2,0:T(8,128)(2,1)S(1)}, u32[]{:S(2)}) copy-start(bf16[1,384,1024]{1,2,0:T(8,128)(2,1)S(1)} %get-tuple-element.33) | copy-start | bytes 2359300
  29.9 0.9 copy-start.8
  35.8 3.0 %copy-start.7 = (bf16[1,384,1024]{1,2,0:T(8,128)(2,1)S(1)}, bf16[1,384,1024]{1,2,0:T(8,128)(2,1)}, u32[]{:S(2)}) copy-start(bf16[1,384,1024]{1,2,0:T(8,128)(2,1)} %copy-done.6) | copy-start | bytes 2359300
  35.8 3.0 %copy-start.15 = (bf16[128,1024]{0,1:T(8,128)(2,1)S(1)}, bf16[128,1024]{0,1:T(8,128)(2,1)}, u32[]{:S(2)}) copy-start(bf16[128,1024]{0,1:T(8,128)(2,1)} %copy.86) | copy-start | bytes 786436
  35.8 3.0 %copy-start.18 = (f32[8,384,128]{2,1,0:T(8,128)S(1)}, f32[8,384,128]{2,1,0:T(8,128)}, u32[]{:S(2)}) copy-start(f32[8,384,128]{2,1,0:T(8,128)} %get-tuple-element.39) | copy-start | bytes 4718596
  38.8 1.0 copy-start.14
  39.8 1.7 %copy-start.4 = (bf16[8,128,384]{1,2,0:T(8,128)(2,1)}, bf16[8,128,384]{1,2,0:T(8,128)(2,1)S(1)}, u32[]{:S(2)}) copy-start(bf16[8,128,384]{1,2,0:T(8,128)(2,1)S(1)} %fusion.10) | copy-start | bytes 2359300
  52.2 4.5 %copy-start.11 = (f32[1,128,1024]{2,1,0:T(8,128)S(1)}, f32[1,128,1024]{2,1,0:T(8,128)}, u32[]{:S(2)}) copy-start(f32[1,128,1024]{2,1,0:T(8,128)} %copy.74) | copy-start | bytes 1572868
  52.2 4.5 %copy-start.12 = (f32[1,128,1024]{2,1,0:T(8,128)S(1)}, f32[1,128,1024]{2,1,0:T(8,128)}, u32[]{:S(2)}) copy-start(f32[1,128,1024]{2,1,0:T(8,128)} %copy.75) | copy-start | bytes 1572868
  54.6 4.5 %copy-start.3 = (bf16[1,384,1024]{1,2,0:T(8,128)(2,1)S(1)}, bf16[1,384,1024]{1,2,0:T(8,128)(2,1)}, u32[]{:S(2)}) copy-start(bf16[1,384,1024]{1,2,0:T(8,128)(2,1)} %copy-done.2) | copy-start | bytes 2359300
  54.6 4.5 %copy-start.5 = (bf16[8,128,384]{1,2,0:T(8,128)(2,1)S(1)}, bf16[8,128,384]{1,2,0:T(8,128)(2,1)}, u32[]{:S(2)}) copy-start(bf16[8,128,384]{1,2,0:T(8,128)(2,1)} %copy-done.4) | copy-start | bytes 2359300
  54.6 95.5 %collective-permute-start.2 = (f32[2,128,1024]{2,1,0:T(8,128)}, f32[2,128,1024]{2,1,0:T(8,128)}, u32[]{:S(2)}, u32[]{:S(2)}) collective-permute-start(f32[2,128,1024]{2,1,0:T(8,128)} %pad_maximum_fusion.1), channel_id=1, source_target_pairs={{8,0},{16,8},{24,16},{32,24},{40,32},{48,40},{56,48},{64,56},{72,6... | collective-permute-start | bytes 3145736 | tf_op jit(solution)/shard_map/ppermute | solution.py:20
  57.8 92.3 %collective-permute-start.3 = (f32[2,128,1024]{2,1,0:T(8,128)}, f32[2,128,1024]{2,1,0:T(8,128)}, u32[]{:S(2)}, u32[]{:S(2)}) collective-permute-start(f32[2,128,1024]{2,1,0:T(8,128)} %pad_maximum_fusion.2), channel_id=1, source_target_pairs={{16,0},{24,8},{32,16},{40,24},{48,32},{56,40},{64,48},{72,56},{80,... | collective-permute-start | bytes 3145736 | tf_op jit(solution)/shard_map/ppermute | solution.py:20
  148.8 1.2 copy-start.9
  148.8 1.2 copy-start.10

commit v2 on v0

v2 whole, which is shorter than its diff:
```python
import functools

import jax
import jax.numpy as jnp
from jax import lax
from jax.experimental import pallas as pl
from jax.experimental.pallas import tpu as pltpu
from jax.sharding import PartitionSpec as P

HEADS = 8
WINDOW = 256
NX, NY, NZ = 4, 8, 12
OWNERS = 8
NSEQ = NX * NZ * 2
MESH = pl.DeviceIdType.MESH
f32, bf16 = jnp.float32, jnp.bfloat16
LAST = (((1,), (1,)), ((), ()))
FIRST = (((0,), (0,)), ((), ()))


def dot(a, b, dims=(((1,), (0,)), ((), ()))):
    return lax.dot_general(a, b, dims, preferred_element_type=f32)


def layer_kernel(
    token_total, len_ref, q_hbm, k_hbm, v_hbm, u_hbm, og_hbm, w_hbm,
    out_ref, gq_ref, gk_ref, gv_ref, gg_ref, gw_ref,
    q, u, w, og8, kwin, vwin, maskf, slope, att, mixed, gh, gmix, inv, hid, ht, htr, gs, ry, s2, rz, ag, finr, go, pg, rg,
    ld_sem, ss_kv, rs_kv, ss_og, rs_og, ss_h, rs_h, ss_y, rs_y, ss_z, rs_z, ss_a, rs_a, ss_f, rs_f, ss_g, rs_g,
):
    seq = lax.axis_index("seq")
    y = lax.axis_index("batch")
    k = lax.rem(seq, 2)
    x = seq // (2 * NZ)
    z = lax.rem(seq // 2, NZ)
    me = x * 2 + k

    def dev(px, py, pz, pk):
        return {"seq": (px * NZ + pz) * 2 + pk, "batch": py}

    def ring(d):
        return {"seq": lax.rem(seq + d + NSEQ, NSEQ), "batch": y}

    partner = dev(x, y, z, 1 - k)
    xs = [dev(lax.rem(x + d, NX), y, z, k) for d in range(1, NX)]
    xo = [dev(lax.rem(x + d, NX), y, z, 1 - k) for d in range(1, NX)]
    ys = [dev(x, lax.rem(y + d, NY), z, k) for d in range(1, NY)]
    zs = [dev(x, y, lax.rem(z + d, NZ), k) for d in range(1, NZ)]
    xk = [partner] + xs + xo
    to_slab = [x * 2 + 1 - k] + [lax.rem(x + d, NX) * 2 + k for d in range(1, NX)] + [lax.rem(x + d, NX) * 2 + 1 - k for d in range(1, NX)]
    hops = [ring(-1), ring(1), ring(-2), ring(2)]

    barrier = pltpu.get_barrier_semaphore()
    greeted = xk + ys + zs + hops
    for peer in greeted:
        pl.semaphore_signal(barrier, inc=1, device_id=peer, device_id_type=MESH)

    def remote(src, dst, ss, rs, peer):
        return pltpu.make_async_remote_copy(src_ref=src, dst_ref=dst, send_sem=ss, recv_sem=rs, device_id=peer, device_id_type=MESH)

    def lanes(h):
        return pl.ds(pl.multiple_of(h * 128, 128), 128)

    loads = [
        pltpu.make_async_copy(q_hbm.at[0], q, ld_sem.at[0]),
        pltpu.make_async_copy(og_hbm.at[0], og8.at[me], ld_sem.at[1]),
        pltpu.make_async_copy(w_hbm, w, ld_sem.at[2]),
        pltpu.make_async_copy(u_hbm.at[0], u, ld_sem.at[3]),
    ]
    for h in range(HEADS):
        loads.append(pltpu.make_async_copy(k_hbm.at[0, :, pl.ds(h * 128, 128)], kwin.at[h, pl.ds(256, 128)], ld_sem.at[4 + 2 * h]))
        loads.append(pltpu.make_async_copy(v_hbm.at[0, :, pl.ds(h * 128, 128)], vwin.at[h, pl.ds(256, 128)], ld_sem.at[5 + 2 * h]))
    for c in loads:
        c.start()
    pl.semaphore_wait(barrier, len(greeted))

    def kv_far(h, which):
        src, dst = ((k_hbm, kwin), (v_hbm, vwin))[which]
        return remote(src.at[0, :, lanes(h)], dst.at[h, pl.ds(0, 128)], ss_kv.at[0, h, which], rs_kv.at[0, h, which], ring(2))

    def kv_near(h, which):
        src, dst = ((k_hbm, kwin), (v_hbm, vwin))[which]
        return remote(src.at[0, :, lanes(h)], dst.at[h, pl.ds(128, 128)], ss_kv.at[1, h, which], rs_kv.at[1, h, which], partner)

    def kv_relay(h, which):
        dst = (kwin, vwin)[which]
        return remote(dst.at[h, pl.ds(0, 128)], dst.at[h, pl.ds(128, 128)], ss_kv.at[1, h, which], rs_kv.at[1, h, which], partner)

    for h in range(HEADS):
        for which in range(2):
            kv_far(h, which).start()

    @pl.when(k == 0)
    def _():
        for h in range(HEADS):
            for which in range(2):
                kv_near(h, which).start()

    og_sends = [remote(og_hbm.at[0], og8.at[me], ss_og.at[d - 1], rs_og.at[d - 1], xs[d - 1]) for d in range(1, NX)]
    og_sends.append(remote(og_hbm.at[0], og8.at[me], ss_og.at[3], rs_og.at[3], partner))
    for c in og_sends:
        c.start()

    loads[1].wait()
    loads[2].wait()
    gh[...] = dot(og8[me], w[...], LAST)
    b1 = len_ref[0, 0]
    b2 = b1 + len_ref[0, 1]
    b3 = b2 + len_ref[0, 2]
    base = seq * 128
    pos = base + lax.broadcasted_iota(jnp.int32, (128, 384), 0)
    key_pos = base - 256 + lax.broadcasted_iota(jnp.int32, (128, 384), 1)
    start = jnp.where(pos >= b3, b3, jnp.where(pos >= b2, b2, jnp.where(pos >= b1, b1, 0)))
    allowed = (key_pos >= start) & (key_pos <= pos) & (key_pos > pos - WINDOW)
    maskf[...] = jnp.where(allowed, 1.0, 0.0)
    loads[0].wait()
    for c in loads[3:]:
        c.wait()
    scale = 128 ** (-0.5)

    def forward(h, carry):
        for which in range(2):
            kv_far(h, which).wait_recv()

        @pl.when(k == 1)
        def _():
            for which in range(2):
                kv_relay(h, which).start()

        for which in range(2):
            kv_near(h, which).wait_recv()
        s = dot(q[:, lanes(h)], kwin[h], LAST) * scale
        g = 1.0 / (1.0 + jnp.exp(-s))
        ok = maskf[...] > 0.0
        a = jnp.where(ok, s * g, 0.0).astype(bf16)
        att[h] = a
        slope[h] = jnp.where(ok, g * (1.0 + s * (1.0 - g)) * scale, 0.0)
        mixed[:, lanes(h)] = dot(a, vwin[h])
        return carry

    lax.fori_loop(0, HEADS, forward, 0)

    relays = []
    for d in range(1, NX):
        slot = lax.rem(x - d + NX, NX) * 2 + k
        og_sends[d - 1].wait_recv()
        relays.append(remote(og8.at[slot], og8.at[slot], ss_og.at[3 + d], rs_og.at[3 + d], partner))
        relays[-1].start()

    def norm(i, carry):
        rows = pl.ds(pl.multiple_of(i * 16, 16), 16)
        m = mixed[rows, :]
        c = m - jnp.mean(m, axis=1, keepdims=True)
        r = lax.rsqrt(jnp.mean(c * c, axis=1, keepdims=True) + 1e-05)
        n = c * r
        mixed[rows, :] = n
        inv[rows, :] = jnp.broadcast_to(r, (16, 128))
        hid[rows, :] = (n * u[rows, :].astype(f32)).astype(bf16)
        return carry

    lax.fori_loop(0, 8, norm, 0)

    for i in range(NY):
        ht[:, i] = hid[:, i * 128:i * 128 + 128].T.reshape(8, 16, 128)
    h_sends = [remote(ht.at[to_slab[r]], htr.at[me], ss_h.at[r], rs_h.at[r], xk[r]) for r in range(7)]
    for c in h_sends:
        c.start()
    htr[me] = ht[me]

    def norm_back(i, carry):
        rows = pl.ds(pl.multiple_of(i * 16, 16), 16)
        n = mixed[rows, :]
        g = gh[rows, :]
        gg_ref[rows, :] = (g * n).astype(bf16)
        gn = g * u[rows, :].astype(f32)
        gm = gn - jnp.mean(gn, axis=1, keepdims=True) - n * jnp.mean(gn * n, axis=1, keepdims=True)
        gmix[rows, :] = (gm * inv[rows, 0:1]).astype(bf16)
        return carry

    lax.fori_loop(0, 8, norm_back, 0)

    def grad_send(b, h):
        return remote(pg.at[b, h], rg.at[b, h], ss_g.at[b, h], rs_g.at[b, h], ring(-1 - b))

    def backward(h, carry):
        gm = gmix[:, lanes(h)]
        da = dot(gm, vwin[h], LAST)
        ds = (da * slope[h]).astype(bf16)
        gq_ref[:, lanes(h)] = dot(ds, kwin[h]).astype(bf16)
        gk = dot(ds, q[:, lanes(h)], FIRST)
        gv = dot(att[h], gm, FIRST)
        for which, val in enumerate((gk, gv)):
            pg[1, h, which] = val[0:128].astype(bf16)
            pg[0, h, which] = val[128:256].astype(bf16)
            go[h, which] = val[256:384]
        for b in range(2):
            grad_send(b, h).start()
        return carry

    lax.fori_loop(0, 2, backward, 0)

    for c in og_sends[3:]:
        c.wait_recv()
    for c in relays:
        c.wait_recv()
    for c in h_sends:
        c.wait_recv()
    lhs = jnp.concatenate([htr[s].reshape(128, 128) for s in range(8)], axis=1)
    for j in range(4):
        cols = slice(j * 256, j * 256 + 256)
        t = dot(lhs, og8[:, :, cols].reshape(1024, 256))
        gs[:, :, cols] = t.reshape(NY, 16, 256).astype(bf16)
    y_sends = [remote(gs.at[lax.rem(y + d, NY)], ry.at[d - 1], ss_y.at[d - 1], rs_y.at[d - 1], ys[d - 1]) for d in range(1, NY)]
    for c in y_sends:
        c.start()

    lax.fori_loop(2, 6, backward, 0)
    for c in y_sends:
        c.wait_recv()
    t = gs[y].astype(f32)
    for d in range(NY - 1):
        t = t + ry[d].astype(f32)
    for p in range(OWNERS):
        s2[p] = t[:, p * 128:p * 128 + 128].astype(bf16)

    def z_send(d):
        return remote(s2.at[lax.rem(z + d, NZ)], rz.at[d - 1], ss_z.at[d - 1], rs_z.at[d - 1], zs[d - 1])

    def a_send(d):
        return remote(ag.at[z], ag.at[z], ss_a.at[d - 1], rs_a.at[d - 1], zs[d - 1])

    for d in range(1, NZ):
        @pl.when(lax.rem(z + d, NZ) < OWNERS)
        def _():
            z_send(d).start()

    lax.fori_loop(6, HEADS, backward, 0)
    out_ref[...] = dot(hid[...], w[...]).astype(bf16)

    @pl.when(z < OWNERS)
    def _():
        for d in range(1, NZ):
            z_send(d).wait_recv()
        t = s2[z].astype(f32)
        for d in range(NZ - 1):
            t = t + rz[d].astype(f32)
        ag[z] = t.astype(bf16)
        for d in range(1, NZ):
            a_send(d).start()

    for d in range(1, NZ):
        @pl.when(lax.rem(z - d + NZ, NZ) < OWNERS)
        def _():
            a_send(d).wait_recv()

    f_sends = [remote(ag.at[pl.ds(0, OWNERS)], finr.at[me], ss_f.at[r], rs_f.at[r], xk[r]) for r in range(7)]
    for c in f_sends:
        c.start()
    finr[me] = ag[0:OWNERS]

    def grads(h, carry):
        for b in range(2):
            grad_send(b, h).wait_recv()
        gk_ref[:, lanes(h)] = (go[h, 0] + rg[0, h, 0].astype(f32) + rg[1, h, 0].astype(f32)).astype(bf16)
        gv_ref[:, lanes(h)] = (go[h, 1] + rg[0, h, 1].astype(f32) + rg[1, h, 1].astype(f32)).astype(bf16)
        return carry

    lax.fori_loop(0, HEADS, grads, 0)

    for c in f_sends:
        c.wait_recv()
    w_scale = token_total ** (-0.5)
    for s in range(8):
        for p in range(OWNERS):
            gw_ref[s * 16:s * 16 + 16, p * 128:p * 128 + 128] = finr[s, p].astype(f32) * w_scale

    def drain(h, carry):
        for which in range(2):
            kv_far(h, which).wait_send()
            kv_near(h, which).wait_send()
        for b in range(2):
            grad_send(b, h).wait_send()
        return carry

    lax.fori_loop(0, HEADS, drain, 0)
    for c in og_sends + relays + h_sends + y_sends + f_sends:
        c.wait_send()
    for d in range(1, NZ):
        @pl.when(lax.rem(z + d, NZ) < OWNERS)
        def _():
            z_send(d).wait_send()

    @pl.when(z < OWNERS)
    def _():
        for d in range(1, NZ):
            a_send(d).wait_send()


def on_device(queries, keys, values, gates, out_grad, w_out, hist_lengths):
    vm = pltpu.VMEM
    dma = pltpu.SemaphoreType.DMA
    rows, width = 128, 1024
    token_total = rows * lax.axis_size("seq") * lax.axis_size("batch")
    hbm = pl.BlockSpec(memory_space=pl.ANY)
    res = pl.BlockSpec(memory_space=pltpu.VMEM)
    outs = pl.pallas_call(
        functools.partial(layer_kernel, token_total),
        out_shape=[jax.ShapeDtypeStruct((rows, width), bf16)] * 5 + [jax.ShapeDtypeStruct((rows, width), f32)],
        in_specs=[pl.BlockSpec(memory_space=pltpu.SMEM)] + [hbm] * 6,
        out_specs=[res] * 6,
        scratch_shapes=[
            vm((rows, width), bf16), vm((rows, width), bf16), vm((width, width), bf16), vm((8, rows, width), bf16),
            vm((HEADS, 384, 128), bf16), vm((HEADS, 384, 128), bf16), vm((128, 384), f32),
            vm((HEADS, 128, 384), f32), vm((HEADS, 128, 384), bf16),
            vm((rows, width), f32), vm((rows, width), f32), vm((rows, width), bf16), vm((rows, 128), f32), vm((rows, width), bf16),
            vm((8, NY, 16, 128), bf16), vm((8, NY, 16, 128), bf16),
            vm((NY, 16, width), bf16), vm((NY - 1, 16, width), bf16),
            vm((NZ, 16, 128), bf16), vm((NZ - 1, 16, 128), bf16), vm((NZ, 16, 128), bf16),
            vm((8, OWNERS, 16, 128), bf16),
            vm((HEADS, 2, 128, 128), f32), vm((2, HEADS, 2, 128, 128), bf16), vm((2, HEADS, 2, 128, 128), bf16),
            dma((20,)), dma((2, HEADS, 2)), dma((2, HEADS, 2)), dma((7,)), dma((7,)), dma((7,)), dma((7,)),
            dma((NY - 1,)), dma((NY - 1,)), dma((NZ - 1,)), dma((NZ - 1,)), dma((NZ - 1,)), dma((NZ - 1,)),
            dma((7,)), dma((7,)), dma((2, HEADS)), dma((2, HEADS)),
        ],
        compiler_params=pltpu.CompilerParams(collective_id=0, has_side_effects=True, vmem_limit_bytes=56 << 20),
    )(hist_lengths, queries, keys, values, gates, out_grad, w_out)
    return tuple(o[None] for o in outs[:5]) + (outs[5],)


def solution(mesh):
    tokens = P("batch", "seq", None)
    return jax.shard_map(
        on_device,
        mesh=mesh,
        in_specs=(tokens,) * 5 + (P(), P("batch", None)),
        out_specs=(tokens,) * 5 + (P("batch", None),),
        check_vma=False,
    )
```

time: 392 us -> 91.8 us (0.23)
  waiting for transfers between devices: 322 us -> 0 us
  Pallas kernels: 0 us -> 82.6 us
  between operations: 14.4 us -> 0.66 us
  matrix products: 13.3 us -> 0 us
  starting transfers between devices: 11.4 us -> 0 us
  local copies, waits for them, and re-layouts: 19.6 us -> 8.25 us
  other arithmetic: 10.9 us -> 0 us
    psum x1 -> x0, waiting for transfers between devices: 271 us -> none  [on_device(): grad_weight = lax.psum(weight_share, 'seq') * token_total ** (-0.5)]
    pallas_call x0 -> x1, Pallas kernels: none -> 82.6 us  [on_device(): pl.pallas_call(functools.partial(layer_kernel, token_total), out_shape=[j...]
    reduce_scatter x1 -> x0, waiting for transfers between devices: 37.6 us -> none  [on_device(): lax.psum_scatter(lax.dot_general(hidden, grad_rows, (((0,), (0,)), ((), (...]
    dot_general x9 -> x0, matrix products: 13.3 us -> none  [the longest x1 2.67 us: on_device(): jnp.einsum('ihe,jhe->hij', mix_heads, value_heads, preferred_element_type...]
    ppermute x4 -> x0, waiting for transfers between devices: 13 us -> none  [shifted(): return lax.ppermute(block, axis, route)]
    ppermute x4 -> x0, starting transfers between devices: 11.4 us -> none  [shifted(): return lax.ppermute(block, axis, route)]
    another operation x7 -> x0, local copies, waits for them, and re-layouts: 10.9 us -> none  [the longest x4 7.4 us: on_device(): jnp.stack((grad_key_all[distance * row_total:(distance + 1) * row_total],...]
    another operation x5 -> x0, other arithmetic: 6.35 us -> none  [the longest x2 3.44 us: on_device(): jnp.stack((grad_key_all[distance * row_total:(distance + 1) * row_total],...]
  transfers between devices with their start and end apart: 6 -> 0, of which waited for: 4 -> 0; matrix products, arithmetic and copies ran while one was open for 8% -> 0% of each run, Pallas kernels for 0% -> 0%
where the time goes in v2:
time: 91.8 us; the launch traced here: 91.6 us
  Pallas kernels  82.6 us (90%)
  local copies, waits for them, and re-layouts  8.25 us (9%)
    pallas_call x1, Pallas kernels, on_device(): pl.pallas_call(functools.partial(layer_kernel, token_total), out_shape=[j...  82.6 us
    unnamed x10, local copies, waits for them, and re-layouts  8.25 us

profile of v2, /device:TPU:1, one launch (start us, length us, event | category | flops | bytes accessed | tf_op | source)
XLA Modules:
  0.0 91.6 jit_solution(7740366321222069610)
XLA Ops:
  0.6 82.6 %shard_map.118 = (bf16[128,1024]{1,0:T(8,128)(2,1)}, bf16[128,1024]{1,0:T(8,128)(2,1)}, bf16[128,1024]{1,0:T(8,128)(2,1)}, bf16[128,1024]{1,0:T(8,128)(2,1)}, bf...) custom-call(s32[1,4]{1,0:T(1,128)} %len_ref.1, bf16[1,128,1024]{2,1,0:T(8,128)(2,1)} %q_hbm.1, bf16[1,128,1024]{2,1,0:T(8,128)(2,1)} %k_hbm.1, ...), custom_call_target="tpu_custom_call" | custom-call | tf_op jit(solution)/shard_map/pallas_call | solution.py:306
  83.3 0.0 copy-start.1
  83.3 0.0 copy-start
  83.3 1.7 %copy.19 = bf16[1,128,1024]{2,1,0:T(8,128)(2,1)} copy(bf16[1,128,1024]{2,1,0:T(8,128)(2,1)} %bitcast.9) | data formatting | bytes 524288
  85.0 1.7 %copy.20 = bf16[1,128,1024]{2,1,0:T(8,128)(2,1)} copy(bf16[1,128,1024]{2,1,0:T(8,128)(2,1)} %bitcast.8) | data formatting | bytes 524288
  86.7 1.7 %copy.21 = bf16[1,128,1024]{2,1,0:T(8,128)(2,1)} copy(bf16[1,128,1024]{2,1,0:T(8,128)(2,1)} %bitcast.7) | data formatting | bytes 524288
  88.4 1.7 %copy.22 = bf16[1,128,1024]{2,1,0:T(8,128)(2,1)} copy(bf16[1,128,1024]{2,1,0:T(8,128)(2,1)} %bitcast.6) | data formatting | bytes 524288
  90.1 0.0 copy-done.1
  90.1 0.7 copy.23
  90.8 0.0 copy-done
  90.8 0.8 copy.24
Async XLA Ops:
  83.3 6.8 %copy-start.1 = (bf16[128,1024]{1,0:T(8,128)(2,1)S(1)}, bf16[128,1024]{1,0:T(8,128)(2,1)}, u32[]{:S(2)}) copy-start(bf16[128,1024]{1,0:T(8,128)(2,1)} %get-tuple-element.16) | copy-start | bytes 786436
  83.3 7.5 %copy-start = (f32[128,1024]{1,0:T(8,128)S(1)}, f32[128,1024]{1,0:T(8,128)}, u32[]{:S(2)}) copy-start(f32[128,1024]{1,0:T(8,128)} %get-tuple-element.29) | copy-start | bytes 1572868

commit v3 on v2

--- a/solution.py
+++ b/solution.py
@@ -25,7 +25,7 @@
 def layer_kernel(
     token_total, len_ref, q_hbm, k_hbm, v_hbm, u_hbm, og_hbm, w_hbm,
     out_ref, gq_ref, gk_ref, gv_ref, gg_ref, gw_ref,
-    q, u, w, og8, kwin, vwin, maskf, slope, att, mixed, gh, gmix, inv, hid, ht, htr, gs, ry, s2, rz, ag, finr, go, pg, rg,
+    q, u, w, og8, kwin, vwin, maskf, slope, att, mixed, gh, gmix, inv, hid, ht, htr, gs, ry, s2, rz, ag, finr, go, far, pg, rg,
     ld_sem, ss_kv, rs_kv, ss_og, rs_og, ss_h, rs_h, ss_y, rs_y, ss_z, rs_z, ss_a, rs_a, ss_f, rs_f, ss_g, rs_g,
 ):
     seq = lax.axis_index("seq")
@@ -43,11 +43,14 @@
 
     partner = dev(x, y, z, 1 - k)
     xs = [dev(lax.rem(x + d, NX), y, z, k) for d in range(1, NX)]
-    xo = [dev(lax.rem(x + d, NX), y, z, 1 - k) for d in range(1, NX)]
+
+    def slab_peer(r):
+        s = lax.rem(me + r, 8)
+        return s, dev(s // 2, y, z, lax.rem(s, 2))
+
     ys = [dev(x, lax.rem(y + d, NY), z, k) for d in range(1, NY)]
     zs = [dev(x, y, lax.rem(z + d, NZ), k) for d in range(1, NZ)]
-    xk = [partner] + xs + xo
-    to_slab = [x * 2 + 1 - k] + [lax.rem(x + d, NX) * 2 + k for d in range(1, NX)] + [lax.rem(x + d, NX) * 2 + 1 - k for d in range(1, NX)]
+    xk = [slab_peer(r)[1] for r in range(1, 8)]
     hops = [ring(-1), ring(1), ring(-2), ring(2)]
 
     barrier = pltpu.get_barrier_semaphore()
@@ -75,17 +78,19 @@
     pl.semaphore_wait(barrier, len(greeted))
 
     def kv_far(h, which):
-        src, dst = ((k_hbm, kwin), (v_hbm, vwin))[which]
-        return remote(src.at[0, :, lanes(h)], dst.at[h, pl.ds(0, 128)], ss_kv.at[0, h, which], rs_kv.at[0, h, which], ring(2))
+        ref = (kwin, vwin)[which]
+        return remote(ref.at[h, pl.ds(256, 128)], ref.at[h, pl.ds(0, 128)], ss_kv.at[0, h, which], rs_kv.at[0, h, which], ring(2))
 
     def kv_near(h, which):
-        src, dst = ((k_hbm, kwin), (v_hbm, vwin))[which]
-        return remote(src.at[0, :, lanes(h)], dst.at[h, pl.ds(128, 128)], ss_kv.at[1, h, which], rs_kv.at[1, h, which], partner)
+        ref = (kwin, vwin)[which]
+        return remote(ref.at[h, pl.ds(256, 128)], ref.at[h, pl.ds(128, 128)], ss_kv.at[1, h, which], rs_kv.at[1, h, which], partner)
 
     def kv_relay(h, which):
         dst = (kwin, vwin)[which]
         return remote(dst.at[h, pl.ds(0, 128)], dst.at[h, pl.ds(128, 128)], ss_kv.at[1, h, which], rs_kv.at[1, h, which], partner)
 
+    for c in loads[4:]:
+        c.wait()
     for h in range(HEADS):
         for which in range(2):
             kv_far(h, which).start()
@@ -96,10 +101,25 @@
             for which in range(2):
                 kv_near(h, which).start()
 
-    og_sends = [remote(og_hbm.at[0], og8.at[me], ss_og.at[d - 1], rs_og.at[d - 1], xs[d - 1]) for d in range(1, NX)]
-    og_sends.append(remote(og_hbm.at[0], og8.at[me], ss_og.at[3], rs_og.at[3], partner))
-    for c in og_sends:
-        c.start()
+    def og_rows(c):
+        return pl.ds(pl.multiple_of(c * 16, 16), 16)
+
+    def og_send(d, c):
+        return remote(og_hbm.at[0, og_rows(c)], og8.at[me, og_rows(c)], ss_og.at[d, c], rs_og.at[d, c], xs[d - 1] if d else partner)
+
+    def og_block(d, c):
+        return og8.at[lax.rem(x - d + NX, NX) * 2 + k, og_rows(c)]
+
+    def og_pass(c):
+        return remote(og_block(3, c), og_block(3, c), ss_og.at[2, c], rs_og.at[2, c], xs[2])
+
+    def og_relay(d, c):
+        return remote(og_block(d, c), og_block(d, c), ss_og.at[3 + d, c], rs_og.at[3 + d, c], partner)
+
+    for c in range(8):
+        og_send(3, c).start()
+    for c in range(8):
+        og_send(0, c).start()
 
     loads[1].wait()
     loads[2].wait()
@@ -114,8 +134,7 @@
     allowed = (key_pos >= start) & (key_pos <= pos) & (key_pos > pos - WINDOW)
     maskf[...] = jnp.where(allowed, 1.0, 0.0)
     loads[0].wait()
-    for c in loads[3:]:
-        c.wait()
+    loads[3].wait()
     scale = 128 ** (-0.5)
 
     def forward(h, carry):
@@ -136,36 +155,56 @@
         att[h] = a
         slope[h] = jnp.where(ok, g * (1.0 + s * (1.0 - g)) * scale, 0.0)
         mixed[:, lanes(h)] = dot(a, vwin[h])
+
+        og_send(3, h).wait_recv()
+        og_pass(h).start()
+        og_relay(3, h).start()
+
+        @pl.when(h >= 2)
+        def _():
+            og_pass(h - 2).wait_recv()
+            og_relay(2, h - 2).start()
+
+        @pl.when((h >= 2) & (h < 6))
+        def _():
+            og_send(1, 2 * h - 4).start()
+            og_send(1, 2 * h - 3).start()
+
         return carry
 
     lax.fori_loop(0, HEADS, forward, 0)
 
-    relays = []
-    for d in range(1, NX):
-        slot = lax.rem(x - d + NX, NX) * 2 + k
-        og_sends[d - 1].wait_recv()
-        relays.append(remote(og8.at[slot], og8.at[slot], ss_og.at[3 + d], rs_og.at[3 + d], partner))
-        relays[-1].start()
-
-    def norm(i, carry):
-        rows = pl.ds(pl.multiple_of(i * 16, 16), 16)
-        m = mixed[rows, :]
-        c = m - jnp.mean(m, axis=1, keepdims=True)
-        r = lax.rsqrt(jnp.mean(c * c, axis=1, keepdims=True) + 1e-05)
-        n = c * r
-        mixed[rows, :] = n
-        inv[rows, :] = jnp.broadcast_to(r, (16, 128))
-        hid[rows, :] = (n * u[rows, :].astype(f32)).astype(bf16)
-        return carry
-
-    lax.fori_loop(0, 8, norm, 0)
-
-    for i in range(NY):
-        ht[:, i] = hid[:, i * 128:i * 128 + 128].T.reshape(8, 16, 128)
-    h_sends = [remote(ht.at[to_slab[r]], htr.at[me], ss_h.at[r], rs_h.at[r], xk[r]) for r in range(7)]
-    for c in h_sends:
-        c.start()
+    heads = [slice(h * 128, h * 128 + 128) for h in range(HEADS)]
+    total = mixed[:, heads[0]]
+    for h in heads[1:]:
+        total = total + mixed[:, h]
+    mean = jnp.broadcast_to(jnp.sum(total, axis=1, keepdims=True) * (1.0 / 1024), (128, 128))
+    total = jnp.zeros((128, 128), f32)
+    for h in heads:
+        c = mixed[:, h] - mean
+        total = total + c * c
+    r = jnp.broadcast_to(lax.rsqrt(jnp.sum(total, axis=1, keepdims=True) * (1.0 / 1024) + 1e-05), (128, 128))
+    inv[...] = r
+    for i, h in enumerate(heads):
+        n = (mixed[:, h] - mean) * r
+        mixed[:, h] = n
+        hd = (n * u[:, h].astype(f32)).astype(bf16)
+        hid[:, h] = hd
+        ht[:, i] = hd.T.reshape(8, 16, 128)
+
+    def h_send(r):
+        s, peer = slab_peer(r)
+        return remote(ht.at[s], htr.at[me], ss_h.at[r - 1], rs_h.at[r - 1], peer)
+
+    for r in range(1, 8):
+        h_send(r).start()
     htr[me] = ht[me]
+    for c in (6, 7):
+        og_pass(c).wait_recv()
+        og_relay(2, c).start()
+    for c in range(8):
+        og_send(1, c).wait_recv()
+        og_relay(1, c).start()
 
     def norm_back(i, carry):
         rows = pl.ds(pl.multiple_of(i * 16, 16), 16)
@@ -180,7 +219,7 @@
     lax.fori_loop(0, 8, norm_back, 0)
 
     def grad_send(b, h):
-        return remote(pg.at[b, h], rg.at[b, h], ss_g.at[b, h], rs_g.at[b, h], ring(-1 - b))
+        return remote(pg.at[b, h], rg.at[b, h], ss_g.at[b, h], rs_g.at[b, h], ring(-2) if b else partner)
 
     def backward(h, carry):
         gm = gmix[:, lanes(h)]
@@ -190,21 +229,32 @@
         gk = dot(ds, q[:, lanes(h)], FIRST)
         gv = dot(att[h], gm, FIRST)
         for which, val in enumerate((gk, gv)):
-            pg[1, h, which] = val[0:128].astype(bf16)
             pg[0, h, which] = val[128:256].astype(bf16)
+            far[h, which] = val[0:128]
             go[h, which] = val[256:384]
-        for b in range(2):
-            grad_send(b, h).start()
-        return carry
-
-    lax.fori_loop(0, 2, backward, 0)
-
-    for c in og_sends[3:]:
-        c.wait_recv()
-    for c in relays:
-        c.wait_recv()
-    for c in h_sends:
-        c.wait_recv()
+        grad_send(0, h).start()
+        return carry
+
+    lax.fori_loop(0, HEADS, backward, 0)
+    low = (k == 0).astype(f32)
+    high = (k == 1).astype(f32)
+
+    def combine(h, carry):
+        grad_send(0, h).wait_recv()
+        got = rg[0, h].astype(f32)
+        pg[1, h] = (far[h] + got * high).astype(bf16)
+        go[h] = go[h] + got * low
+        grad_send(1, h).start()
+        return carry
+
+    lax.fori_loop(0, HEADS, combine, 0)
+
+    for c in range(8):
+        og_send(0, c).wait_recv()
+        for d in range(1, NX):
+            og_relay(d, c).wait_recv()
+    for r in range(1, 8):
+        h_send(r).wait_recv()
     lhs = jnp.concatenate([htr[s].reshape(128, 128) for s in range(8)], axis=1)
     for j in range(4):
         cols = slice(j * 256, j * 256 + 256)
@@ -214,7 +264,7 @@
     for c in y_sends:
         c.start()
 
-    lax.fori_loop(2, 6, backward, 0)
+    out_ref[...] = dot(hid[...], w[...]).astype(bf16)
     for c in y_sends:
         c.wait_recv()
     t = gs[y].astype(f32)
@@ -234,8 +284,14 @@
         def _():
             z_send(d).start()
 
-    lax.fori_loop(6, HEADS, backward, 0)
-    out_ref[...] = dot(hid[...], w[...]).astype(bf16)
+    def grads(h, carry):
+        grad_send(1, h).wait_recv()
+        total = go[h] + rg[1, h].astype(f32)
+        gk_ref[:, lanes(h)] = total[0].astype(bf16)
+        gv_ref[:, lanes(h)] = total[1].astype(bf16)
+        return carry
+
+    lax.fori_loop(0, HEADS, grads, 0)
 
     @pl.when(z < OWNERS)
     def _():
@@ -248,27 +304,23 @@
         for d in range(1, NZ):
             a_send(d).start()
 
-    for d in range(1, NZ):
-        @pl.when(lax.rem(z - d + NZ, NZ) < OWNERS)
-        def _():
-            a_send(d).wait_recv()
-
-    f_sends = [remote(ag.at[pl.ds(0, OWNERS)], finr.at[me], ss_f.at[r], rs_f.at[r], xk[r]) for r in range(7)]
-    for c in f_sends:
-        c.start()
-    finr[me] = ag[0:OWNERS]
-
-    def grads(h, carry):
-        for b in range(2):
-            grad_send(b, h).wait_recv()
-        gk_ref[:, lanes(h)] = (go[h, 0] + rg[0, h, 0].astype(f32) + rg[1, h, 0].astype(f32)).astype(bf16)
-        gv_ref[:, lanes(h)] = (go[h, 1] + rg[0, h, 1].astype(f32) + rg[1, h, 1].astype(f32)).astype(bf16)
-        return carry
-
-    lax.fori_loop(0, HEADS, grads, 0)
-
-    for c in f_sends:
-        c.wait_recv()
+    def f_send(r, p):
+        return remote(ag.at[p], finr.at[me, p], ss_f.at[r - 1, p], rs_f.at[r - 1, p], slab_peer(r)[1])
+
+    for d in (0, 1, 11, 2, 10, 3, 9, 4, 8, 5, 7, 6):
+        p = lax.rem(z - d + NZ, NZ)
+
+        @pl.when(p < OWNERS)
+        def _():
+            if d:
+                a_send(d).wait_recv()
+            finr[me, p] = ag[p]
+            for r in range(1, 8):
+                f_send(r, p).start()
+
+    for r in range(1, 8):
+        for p in range(OWNERS):
+            f_send(r, p).wait_recv()
     w_scale = token_total ** (-0.5)
     for s in range(8):
         for p in range(OWNERS):
@@ -280,10 +332,19 @@
             kv_near(h, which).wait_send()
         for b in range(2):
             grad_send(b, h).wait_send()
+        for d in (0, 1, 3):
+            og_send(d, h).wait_send()
+        og_pass(h).wait_send()
+        for d in range(1, NX):
+            og_relay(d, h).wait_send()
+        for r in range(1, 8):
+            f_send(r, h).wait_send()
         return carry
 
     lax.fori_loop(0, HEADS, drain, 0)
-    for c in og_sends + relays + h_sends + y_sends + f_sends:
+    for r in range(1, 8):
+        h_send(r).wait_send()
+    for c in y_sends:
         c.wait_send()
     for d in range(1, NZ):
         @pl.when(lax.rem(z + d, NZ) < OWNERS)
@@ -294,6 +355,18 @@
     def _():
         for d in range(1, NZ):
             a_send(d).wait_send()
+
+
+def finish_kernel(*refs):
+    sems = refs[-1]
+    copies = []
+    for i in range(6):
+        dst = refs[6 + i].at[0] if i < 5 else refs[6 + i]
+        copies.append(pltpu.make_async_copy(refs[i], dst, sems.at[i]))
+    for c in copies:
+        c.start()
+    for c in copies:
+        c.wait()
 
 
 def on_device(queries, keys, values, gates, out_grad, w_out, hist_lengths):
@@ -305,7 +378,7 @@
     res = pl.BlockSpec(memory_space=pltpu.VMEM)
     outs = pl.pallas_call(
         functools.partial(layer_kernel, token_total),
-        out_shape=[jax.ShapeDtypeStruct((rows, width), bf16)] * 5 + [jax.ShapeDtypeStruct((rows, width), f32)],
+        out_shape=[vm((rows, width), bf16)] * 5 + [vm((rows, width), f32)],
         in_specs=[pl.BlockSpec(memory_space=pltpu.SMEM)] + [hbm] * 6,
         out_specs=[res] * 6,
         scratch_shapes=[
@@ -317,14 +390,21 @@
             vm((NY, 16, width), bf16), vm((NY - 1, 16, width), bf16),
             vm((NZ, 16, 128), bf16), vm((NZ - 1, 16, 128), bf16), vm((NZ, 16, 128), bf16),
             vm((8, OWNERS, 16, 128), bf16),
-            vm((HEADS, 2, 128, 128), f32), vm((2, HEADS, 2, 128, 128), bf16), vm((2, HEADS, 2, 128, 128), bf16),
-            dma((20,)), dma((2, HEADS, 2)), dma((2, HEADS, 2)), dma((7,)), dma((7,)), dma((7,)), dma((7,)),
+            vm((HEADS, 2, 128, 128), f32), vm((HEADS, 2, 128, 128), f32), vm((2, HEADS, 2, 128, 128), bf16), vm((2, HEADS, 2, 128, 128), bf16),
+            dma((20,)), dma((2, HEADS, 2)), dma((2, HEADS, 2)), dma((7, 8)), dma((7, 8)), dma((7,)), dma((7,)),
             dma((NY - 1,)), dma((NY - 1,)), dma((NZ - 1,)), dma((NZ - 1,)), dma((NZ - 1,)), dma((NZ - 1,)),
-            dma((7,)), dma((7,)), dma((2, HEADS)), dma((2, HEADS)),
+            dma((7, OWNERS)), dma((7, OWNERS)), dma((2, HEADS)), dma((2, HEADS)),
         ],
         compiler_params=pltpu.CompilerParams(collective_id=0, has_side_effects=True, vmem_limit_bytes=56 << 20),
     )(hist_lengths, queries, keys, values, gates, out_grad, w_out)
-    return tuple(o[None] for o in outs[:5]) + (outs[5],)
+    finals = pl.pallas_call(
+        finish_kernel,
+        out_shape=[jax.ShapeDtypeStruct((1, rows, width), bf16)] * 5 + [jax.ShapeDtypeStruct((rows, width), f32)],
+        in_specs=[hbm] * 6,
+        out_specs=[hbm] * 6,
+        scratch_shapes=[dma((6,))],
+    )(*[pltpu.with_memory_space_constraint(o, pltpu.VMEM) for o in outs])
+    return tuple(finals)
 
 
 def solution(mesh):

time: 91.8 us -> 77.2 us (0.84)
  local copies, waits for them, and re-layouts: 8.25 us -> 0 us
  Pallas kernels: 82.6 us -> 76.4 us
    unnamed x10 -> x0, local copies, waits for them, and re-layouts: 8.25 us -> none
    pallas_call x1 -> x2, Pallas kernels: 82.6 us -> 76.4 us  [the longest x1 75.1 us: on_device(): pl.pallas_call(functools.partial(layer_kernel, token_total), out_shape=[v...]
where the time goes in v3:
time: 77.2 us; the launch traced here: 77.1 us
  Pallas kernels  76.4 us (99%)
    pallas_call x1, Pallas kernels, on_device(): pl.pallas_call(functools.partial(layer_kernel, token_total), out_shape=[v...  75.1 us

profile of v3, /device:TPU:1, one launch (start us, length us, event | category | flops | bytes accessed | tf_op | source)
XLA Modules:
  0.0 77.1 jit_solution(2943740217658795526)
XLA Ops:
  0.6 75.1 %shard_map.118 = (bf16[128,1024]{1,0:T(8,128)(2,1)S(1)}, bf16[128,1024]{1,0:T(8,128)(2,1)S(1)}, bf16[128,1024]{1,0:T(8,128)(2,1)S(1)}, bf16[128,1024]{1,0:T(8,12...) custom-call(s32[1,4]{1,0:T(1,128)} %len_ref.1, bf16[1,128,1024]{2,1,0:T(8,128)(2,1)} %q_hbm.1, ...), custom_call_target="tpu_custom_call" | custom-call | tf_op jit(solution)/shard_map/pallas_call | solution.py:379
  75.8 1.3 %shard_map.119 = (bf16[1,128,1024]{2,1,0:T(8,128)(2,1)}, bf16[1,128,1024]{2,1,0:T(8,128)(2,1)}, bf16[1,128,1024]{2,1,0:T(8,128)(2,1)}, bf16[1,128,1024]{2,1,0:T(...) custom-call(bf16[128,1024]{1,0:T(8,128)(2,1)S(1)} %get-tuple-element.12.refs_0_, ...), custom_call_target="tpu_custom_call" | custom-call | tf_op jit(solution)/shard_map/pallas_call | solution.py:400

commit v4 on v3

--- a/solution.py
+++ b/solution.py
@@ -26,7 +26,7 @@
     token_total, len_ref, q_hbm, k_hbm, v_hbm, u_hbm, og_hbm, w_hbm,
     out_ref, gq_ref, gk_ref, gv_ref, gg_ref, gw_ref,
     q, u, w, og8, kwin, vwin, maskf, slope, att, mixed, gh, gmix, inv, hid, ht, htr, gs, ry, s2, rz, ag, finr, go, far, pg, rg,
-    ld_sem, ss_kv, rs_kv, ss_og, rs_og, ss_h, rs_h, ss_y, rs_y, ss_z, rs_z, ss_a, rs_a, ss_f, rs_f, ss_g, rs_g,
+    news, ld_sem, ss_kv, rs_kv, ss_og, rs_og, ss_h, rs_h, ss_y, rs_y, ss_z, rs_z, ss_a, rs_a, ss_f, rs_f, ss_g, rs_g,
 ):
     seq = lax.axis_index("seq")
     y = lax.axis_index("batch")
@@ -51,10 +51,10 @@
     ys = [dev(x, lax.rem(y + d, NY), z, k) for d in range(1, NY)]
     zs = [dev(x, y, lax.rem(z + d, NZ), k) for d in range(1, NZ)]
     xk = [slab_peer(r)[1] for r in range(1, 8)]
-    hops = [ring(-1), ring(1), ring(-2), ring(2)]
+    sides = [ys[0], ys[NY - 2], zs[0], zs[NZ - 2]]
 
     barrier = pltpu.get_barrier_semaphore()
-    greeted = xk + ys + zs + hops
+    greeted = xk + sides + [ring(-2), ring(2)]
     for peer in greeted:
         pl.semaphore_signal(barrier, inc=1, device_id=peer, device_id_type=MESH)
 
@@ -137,7 +137,19 @@
     loads[3].wait()
     scale = 128 ** (-0.5)
 
+    def spread(t):
+        for peer in sides:
+            pl.semaphore_signal(news.at[t], inc=1, device_id=peer, device_id_type=MESH)
+
     def forward(h, carry):
+        @pl.when((h >= 1) & (h <= 5))
+        def _():
+            pl.semaphore_wait(news.at[h - 1], len(sides))
+
+        @pl.when(h < 5)
+        def _():
+            spread(h)
+
         for which in range(2):
             kv_far(h, which).wait_recv()
 
@@ -391,7 +403,7 @@
             vm((NZ, 16, 128), bf16), vm((NZ - 1, 16, 128), bf16), vm((NZ, 16, 128), bf16),
             vm((8, OWNERS, 16, 128), bf16),
             vm((HEADS, 2, 128, 128), f32), vm((HEADS, 2, 128, 128), f32), vm((2, HEADS, 2, 128, 128), bf16), vm((2, HEADS, 2, 128, 128), bf16),
-            dma((20,)), dma((2, HEADS, 2)), dma((2, HEADS, 2)), dma((7, 8)), dma((7, 8)), dma((7,)), dma((7,)),
+            pltpu.SemaphoreType.REGULAR((5,)), dma((20,)), dma((2, HEADS, 2)), dma((2, HEADS, 2)), dma((7, 8)), dma((7, 8)), dma((7,)), dma((7,)),
             dma((NY - 1,)), dma((NY - 1,)), dma((NZ - 1,)), dma((NZ - 1,)), dma((NZ - 1,)), dma((NZ - 1,)),
             dma((7, OWNERS)), dma((7, OWNERS)), dma((2, HEADS)), dma((2, HEADS)),
         ],

time: 77.2 us -> 75.4 us (0.977)
  Pallas kernels: 76.4 us -> 74.7 us
    pallas_call x1, Pallas kernels: 75.1 us -> 73.4 us  [on_device(): pl.pallas_call(functools.partial(layer_kernel, token_total), out_shape=[v...]
where the time goes in v4:
time: 75.4 us; the launch traced here: 75.3 us
  Pallas kernels  74.7 us (99%)
    pallas_call x1, Pallas kernels, on_device(): pl.pallas_call(functools.partial(layer_kernel, token_total), out_shape=[v...  73.4 us

profile of v4, /device:TPU:1, one launch (start us, length us, event | category | flops | bytes accessed | tf_op | source)
XLA Modules:
  0.0 75.3 jit_solution(7739645723032301542)
XLA Ops:
  0.6 73.4 %shard_map.118 = (bf16[128,1024]{1,0:T(8,128)(2,1)S(1)}, bf16[128,1024]{1,0:T(8,128)(2,1)S(1)}, bf16[128,1024]{1,0:T(8,128)(2,1)S(1)}, bf16[128,1024]{1,0:T(8,12...) custom-call(s32[1,4]{1,0:T(1,128)} %len_ref.1, bf16[1,128,1024]{2,1,0:T(8,128)(2,1)} %q_hbm.1, ...), custom_call_target="tpu_custom_call" | custom-call | tf_op jit(solution)/shard_map/pallas_call | solution.py:391
  74.0 1.3 %shard_map.119 = (bf16[1,128,1024]{2,1,0:T(8,128)(2,1)}, bf16[1,128,1024]{2,1,0:T(8,128)(2,1)}, bf16[1,128,1024]{2,1,0:T(8,128)(2,1)}, bf16[1,128,1024]{2,1,0:T(...) custom-call(bf16[128,1024]{1,0:T(8,128)(2,1)S(1)} %get-tuple-element.12.refs_0_, ...), custom_call_target="tpu_custom_call" | custom-call | tf_op jit(solution)/shard_map/pallas_call | solution.py:412

commit v5 on v4

v5 whole, which is shorter than its diff:
```python
import functools

import jax
import jax.numpy as jnp
from jax import lax
from jax.experimental import pallas as pl
from jax.experimental.pallas import tpu as pltpu
from jax.sharding import PartitionSpec as P

HEADS = 8
WINDOW = 256
NX, NY, NZ = 4, 8, 12
OWNERS = 8
NSEQ = NX * NZ * 2
MESH = pl.DeviceIdType.MESH
f32, bf16 = jnp.float32, jnp.bfloat16
LAST = (((1,), (1,)), ((), ()))
FIRST = (((0,), (0,)), ((), ()))


def dot(a, b, dims=(((1,), (0,)), ((), ()))):
    return lax.dot_general(a, b, dims, preferred_element_type=f32)


def layer_kernel(
    token_total, len_hbm, q_hbm, k_hbm, v_hbm, u_hbm, og_hbm, w_hbm,
    out_ref, gq_ref, gk_ref, gv_ref, gg_ref, gw_ref,
    q, u, w, og8, kwin, vwin, maskf, slope, att, mixed, gh, gmix, inv, hid, ht, htr, gs, ry, s2, rz, ag, finr, go, far, pg, rg,
    len_ref, news, ld_sem, ss_kv, rs_kv, ss_og, rs_og, ss_h, rs_h, ss_y, rs_y, ss_z, rs_z, ss_a, rs_a, ss_f, rs_f, ss_g, rs_g,
):
    seq = lax.axis_index("seq")
    y = lax.axis_index("batch")
    k = lax.rem(seq, 2)
    x = seq // (2 * NZ)
    z = lax.rem(seq // 2, NZ)
    me = x * 2 + k

    def dev(px, py, pz, pk):
        return {"seq": (px * NZ + pz) * 2 + pk, "batch": py}

    def ring(d):
        return {"seq": lax.rem(seq + d + NSEQ, NSEQ), "batch": y}

    partner = dev(x, y, z, 1 - k)
    xs = [dev(lax.rem(x + d, NX), y, z, k) for d in range(1, NX)]

    def slab_peer(r):
        s = lax.rem(me + r, 8)
        return s, dev(s // 2, y, z, lax.rem(s, 2))

    ys = [dev(x, lax.rem(y + d, NY), z, k) for d in range(1, NY)]
    zs = [dev(x, y, lax.rem(z + d, NZ), k) for d in range(1, NZ)]
    xk = [slab_peer(r)[1] for r in range(1, 8)]
    sides = [ys[0], ys[NY - 2], zs[0], zs[NZ - 2]]

    barrier = pltpu.get_barrier_semaphore()
    greeted = xk + sides + [ring(-2), ring(2)]
    for peer in greeted:
        pl.semaphore_signal(barrier, inc=1, device_id=peer, device_id_type=MESH)

    def remote(src, dst, ss, rs, peer):
        return pltpu.make_async_remote_copy(src_ref=src, dst_ref=dst, send_sem=ss, recv_sem=rs, device_id=peer, device_id_type=MESH)

    def lanes(h):
        return pl.ds(pl.multiple_of(h * 128, 128), 128)

    loads = [
        pltpu.make_async_copy(q_hbm.at[0], q, ld_sem.at[0]),
        pltpu.make_async_copy(og_hbm.at[0], og8.at[me], ld_sem.at[1]),
        pltpu.make_async_copy(w_hbm, w, ld_sem.at[2]),
        pltpu.make_async_copy(u_hbm.at[0], u, ld_sem.at[3]),
        pltpu.make_async_copy(len_hbm, len_ref, ld_sem.at[5]),
    ]
    for h in range(HEADS):
        loads.append(pltpu.make_async_copy(k_hbm.at[0, :, pl.ds(h * 128, 128)], kwin.at[h, pl.ds(256, 128)], ld_sem.at[4]))
        loads.append(pltpu.make_async_copy(v_hbm.at[0, :, pl.ds(h * 128, 128)], vwin.at[h, pl.ds(256, 128)], ld_sem.at[4]))
    for c in loads:
        c.start()
    pl.semaphore_wait(barrier, len(greeted))

    def kv_far(h, which):
        ref = (kwin, vwin)[which]
        return remote(ref.at[h, pl.ds(256, 128)], ref.at[h, pl.ds(0, 128)], ss_kv.at[0], rs_kv.at[0, h // 2], ring(2))

    def kv_near(h, which):
        ref = (kwin, vwin)[which]
        return remote(ref.at[h, pl.ds(256, 128)], ref.at[h, pl.ds(128, 128)], ss_kv.at[1], rs_kv.at[1, h // 2], partner)

    def kv_relay(h, which):
        dst = (kwin, vwin)[which]
        return remote(dst.at[h, pl.ds(0, 128)], dst.at[h, pl.ds(128, 128)], ss_kv.at[1], rs_kv.at[1, h // 2], partner)

    pltpu.make_async_copy(pg.at[0], pg.at[1], ld_sem.at[4]).wait()
    def arrived(ref, sem):
        remote(ref, ref, ss_kv.at[0], sem, partner).wait_recv()

    def left(ref, sem):
        remote(ref, ref, sem, rs_kv.at[0, 0], partner).wait_send()

    pair = pg.at[0, pl.ds(0, 2)]
    for h in range(HEADS):
        for which in range(2):
            kv_far(h, which).start()

    @pl.when(k == 0)
    def _():
        for h in range(HEADS):
            for which in range(2):
                kv_near(h, which).start()

    def og_rows(c):
        return pl.ds(pl.multiple_of(c * 32, 32), 32)

    def og_send(d, c):
        return remote(og_hbm.at[0, og_rows(c)], og8.at[me, og_rows(c)], ss_og, rs_og.at[8 if d == 1 else c], xs[d - 1])

    def og_slot(d):
        return lax.rem(x - d + NX, NX) * 2 + k

    def og_pass(c):
        block = og8.at[og_slot(3), og_rows(c)]
        return remote(block, block, ss_og, rs_og.at[4 + c], xs[2])

    def og_relay(d, c):
        block = og8.at[og_slot(d), og_rows(c)]
        return remote(block, block, ss_og, rs_og.at[9], partner)

    for c in range(4):
        og_send(3, c).start()
    remote(og_hbm.at[0], og8.at[me], ss_og, rs_og.at[9], partner).start()

    loads[1].wait()
    loads[2].wait()
    loads[4].wait()
    gh[...] = dot(og8[me], w[...], LAST)
    b1 = len_ref[0, 0]
    b2 = b1 + len_ref[0, 1]
    b3 = b2 + len_ref[0, 2]
    base = seq * 128
    pos = base + lax.broadcasted_iota(jnp.int32, (128, 384), 0)
    key_pos = base - 256 + lax.broadcasted_iota(jnp.int32, (128, 384), 1)
    start = jnp.where(pos >= b3, b3, jnp.where(pos >= b2, b2, jnp.where(pos >= b1, b1, 0)))
    allowed = (key_pos >= start) & (key_pos <= pos) & (key_pos > pos - WINDOW)
    maskf[...] = jnp.where(allowed, 1.0, 0.0)
    loads[0].wait()
    loads[3].wait()
    scale = 128 ** (-0.5)

    def spread(t):
        for peer in sides:
            pl.semaphore_signal(news.at[t], inc=1, device_id=peer, device_id_type=MESH)

    def forward(c, carry):
        @pl.when(c >= 1)
        def _():
            pl.semaphore_wait(news.at[c - 1], len(sides))

        spread(c)
        arrived(pair, rs_kv.at[0, c])

        @pl.when(k == 1)
        def _():
            for i in range(2):
                for which in range(2):
                    kv_relay(2 * c + i, which).start()

        arrived(pair, rs_kv.at[1, c])
        for i in range(2):
            h = 2 * c + i
            s = dot(q[:, lanes(h)], kwin[h], LAST) * scale
            g = 1.0 / (1.0 + jnp.exp(-s))
            ok = maskf[...] > 0.0
            a = jnp.where(ok, s * g, 0.0).astype(bf16)
            att[h] = a
            slope[h] = jnp.where(ok, g * (1.0 + s * (1.0 - g)) * scale, 0.0)
            mixed[:, lanes(h)] = dot(a, vwin[h])
        og_send(3, c).wait_recv()
        og_pass(c).start()
        og_relay(3, c).start()

        @pl.when(c >= 1)
        def _():
            og_pass(c - 1).wait_recv()
            og_relay(2, c - 1).start()

        @pl.when(c >= 2)
        def _():
            og_send(1, 2 * c - 4).start()
            og_send(1, 2 * c - 3).start()

        return carry

    lax.fori_loop(0, 4, forward, 0)
    pl.semaphore_wait(news.at[3], len(sides))
    spread(4)

    heads = [slice(h * 128, h * 128 + 128) for h in range(HEADS)]
    total = mixed[:, heads[0]]
    for h in heads[1:]:
        total = total + mixed[:, h]
    mean = jnp.broadcast_to(jnp.sum(total, axis=1, keepdims=True) * (1.0 / 1024), (128, 128))
    total = jnp.zeros((128, 128), f32)
    for h in heads:
        c = mixed[:, h] - mean
        total = total + c * c
    r = jnp.broadcast_to(lax.rsqrt(jnp.sum(total, axis=1, keepdims=True) * (1.0 / 1024) + 1e-05), (128, 128))
    inv[...] = r
    for i, h in enumerate(heads):
        n = (mixed[:, h] - mean) * r
        mixed[:, h] = n
        hd = (n * u[:, h].astype(f32)).astype(bf16)
        hid[:, h] = hd
        ht[:, i] = hd.T.reshape(8, 16, 128)

    def h_send(r):
        s, peer = slab_peer(r)
        return remote(ht.at[s], htr.at[me], ss_h, rs_h, peer)

    for r in (4, 3, 5, 2, 6, 7, 1):
        h_send(r).start()
    htr[me] = ht[me]
    og_pass(3).wait_recv()
    og_relay(2, 3).start()

    def norm_back(i, carry):
        rows = pl.ds(pl.multiple_of(i * 16, 16), 16)
        n = mixed[rows, :]
        g = gh[rows, :]
        gg_ref[rows, :] = (g * n).astype(bf16)
        gn = g * u[rows, :].astype(f32)
        gm = gn - jnp.mean(gn, axis=1, keepdims=True) - n * jnp.mean(gn * n, axis=1, keepdims=True)
        gmix[rows, :] = (gm * inv[rows, 0:1]).astype(bf16)
        return carry

    lax.fori_loop(0, 8, norm_back, 0)

    def grad_send(b, h):
        return remote(pg.at[b, h], rg.at[b, h], ss_g.at[b], rs_g.at[4 if b else h // 2], ring(-2) if b else partner)

    def backward(h, carry):
        gm = gmix[:, lanes(h)]
        da = dot(gm, vwin[h], LAST)
        ds = (da * slope[h]).astype(bf16)
        gq_ref[:, lanes(h)] = dot(ds, kwin[h]).astype(bf16)
        gk = dot(ds, q[:, lanes(h)], FIRST)
        gv = dot(att[h], gm, FIRST)
        for which, val in enumerate((gk, gv)):
            pg[0, h, which] = val[128:256].astype(bf16)
            far[h, which] = val[0:128]
            go[h, which] = val[256:384]
        grad_send(0, h).start()
        return carry

    lax.fori_loop(0, HEADS, backward, 0)
    arrived(og8.at[0], rs_og.at[8])
    block = og8.at[og_slot(1)]
    remote(block, block, ss_og, rs_og.at[9], partner).start()
    low = (k == 0).astype(f32)
    high = (k == 1).astype(f32)

    def combine(c, carry):
        arrived(pair, rs_g.at[c])
        for i in range(2):
            h = 2 * c + i
            got = rg[0, h].astype(f32)
            pg[1, h] = (far[h] + got * high).astype(bf16)
            go[h] = go[h] + got * low
            grad_send(1, h).start()
        return carry

    lax.fori_loop(0, 4, combine, 0)

    arrived(og8.at[pl.ds(0, 4)], rs_og.at[9])
    arrived(ht.at[pl.ds(0, 7)], rs_h)
    lhs = jnp.concatenate([htr[s].reshape(128, 128) for s in range(8)], axis=1)
    for j in range(4):
        cols = slice(j * 256, j * 256 + 256)
        t = dot(lhs, og8[:, :, cols].reshape(1024, 256))
        gs[:, :, cols] = t.reshape(NY, 16, 256).astype(bf16)
    y_sends = [remote(gs.at[lax.rem(y + d, NY)], ry.at[d - 1], ss_y, rs_y, ys[d - 1]) for d in range(1, NY)]
    for d in (4, 3, 5, 2, 6, 1, 7):
        y_sends[d - 1].start()

    out_ref[...] = dot(hid[...], w[...]).astype(bf16)
    arrived(ry, rs_y)
    t = gs[y].astype(f32)
    for d in range(NY - 1):
        t = t + ry[d].astype(f32)
    for p in range(OWNERS):
        s2[p] = t[:, p * 128:p * 128 + 128].astype(bf16)

    def z_send(d):
        return remote(s2.at[lax.rem(z + d, NZ)], rz.at[d - 1], ss_z, rs_z, zs[d - 1])

    def a_send(d):
        return remote(ag.at[z], ag.at[z], ss_a, rs_a.at[d - 1], zs[d - 1])

    pl.semaphore_wait(news.at[4], len(sides))
    far_first = (6, 5, 7, 4, 8, 3, 9, 2, 10, 1, 11)
    for d in far_first:
        @pl.when(lax.rem(z + d, NZ) < OWNERS)
        def _():
            z_send(d).start()

    arrived(rg.at[1], rs_g.at[4])

    def grads(h, carry):
        total = go[h] + rg[1, h].astype(f32)
        gk_ref[:, lanes(h)] = total[0].astype(bf16)
        gv_ref[:, lanes(h)] = total[1].astype(bf16)
        return carry

    lax.fori_loop(0, HEADS, grads, 0)

    @pl.when(z < OWNERS)
    def _():
        arrived(rz, rs_z)
        t = s2[z].astype(f32)
        for d in range(NZ - 1):
            t = t + rz[d].astype(f32)
        ag[z] = t.astype(bf16)
        for d in far_first:
            a_send(d).start()

    def f_send(r, p):
        return remote(ag.at[p], finr.at[me, p], ss_f, rs_f, slab_peer(r)[1])

    for d in (0, 1, 11, 2, 10, 3, 9, 4, 8, 5, 7, 6):
        p = lax.rem(z - d + NZ, NZ)

        @pl.when(p < OWNERS)
        def _():
            if d:
                a_send(d).wait_recv()
            finr[me, p] = ag[p]
            for r in (4, 3, 5, 2, 6, 7, 1):
                f_send(r, p).start()

    arrived(finr.at[pl.ds(0, 7)], rs_f)
    w_scale = token_total ** (-0.5)
    for s in range(8):
        for p in range(OWNERS):
            gw_ref[s * 16:s * 16 + 16, p * 128:p * 128 + 128] = finr[s, p].astype(f32) * w_scale

    for i in range(2):
        left(pg.at[0], ss_kv.at[i])
        left(pg.at[0], ss_g.at[i])
    left(og8.at[pl.ds(0, 7)], ss_og)
    left(ht.at[pl.ds(0, 7)], ss_h)
    left(gs.at[pl.ds(0, 7)], ss_y)
    left(finr.at[pl.ds(0, 7)], ss_f)

    @pl.when(z < OWNERS)
    def _():
        left(s2.at[pl.ds(0, OWNERS - 1)], ss_z)
        left(s2.at[pl.ds(0, NZ - 1)], ss_a)

    @pl.when(z >= OWNERS)
    def _():
        left(s2.at[pl.ds(0, OWNERS)], ss_z)


def finish_kernel(*refs):
    sems = refs[-1]
    copies = []
    for i in range(6):
        dst = refs[6 + i].at[0] if i < 5 else refs[6 + i]
        copies.append(pltpu.make_async_copy(refs[i], dst, sems.at[i]))
    for c in copies:
        c.start()
    for c in copies:
        c.wait()


def on_device(queries, keys, values, gates, out_grad, w_out, hist_lengths):
    vm = pltpu.VMEM
    dma = pltpu.SemaphoreType.DMA
    rows, width = 128, 1024
    token_total = rows * lax.axis_size("seq") * lax.axis_size("batch")
    hbm = pl.BlockSpec(memory_space=pl.ANY)
    res = pl.BlockSpec(memory_space=pltpu.VMEM)
    outs = pl.pallas_call(
        functools.partial(layer_kernel, token_total),
        out_shape=[vm((rows, width), bf16)] * 5 + [vm((rows, width), f32)],
        in_specs=[hbm] * 7,
        out_specs=[res] * 6,
        scratch_shapes=[
            vm((rows, width), bf16), vm((rows, width), bf16), vm((width, width), bf16), vm((8, rows, width), bf16),
            vm((HEADS, 384, 128), bf16), vm((HEADS, 384, 128), bf16), vm((128, 384), f32),
            vm((HEADS, 128, 384), f32), vm((HEADS, 128, 384), bf16),
            vm((rows, width), f32), vm((rows, width), f32), vm((rows, width), bf16), vm((rows, 128), f32), vm((rows, width), bf16),
            vm((8, NY, 16, 128), bf16), vm((8, NY, 16, 128), bf16),
            vm((NY, 16, width), bf16), vm((NY - 1, 16, width), bf16),
            vm((NZ, 16, 128), bf16), vm((NZ - 1, 16, 128), bf16), vm((NZ, 16, 128), bf16),
            vm((8, OWNERS, 16, 128), bf16),
            vm((HEADS, 2, 128, 128), f32), vm((HEADS, 2, 128, 128), f32), vm((2, HEADS, 2, 128, 128), bf16), vm((2, HEADS, 2, 128, 128), bf16),
            pltpu.SMEM((1, 4), jnp.int32), pltpu.SemaphoreType.REGULAR((5,)), dma((6,)), dma((2,)), dma((2, 4)), dma, dma((10,)), dma, dma,
            dma, dma, dma, dma, dma, dma((NZ - 1,)), dma, dma, dma((2,)), dma((5,)),
        ],
        compiler_params=pltpu.CompilerParams(collective_id=0, has_side_effects=True, vmem_limit_bytes=56 << 20),
    )(hist_lengths, queries, keys, values, gates, out_grad, w_out)
    finals = pl.pallas_call(
        finish_kernel,
        out_shape=[jax.ShapeDtypeStruct((1, rows, width), bf16)] * 5 + [jax.ShapeDtypeStruct((rows, width), f32)],
        in_specs=[hbm] * 6,
        out_specs=[hbm] * 6,
        scratch_shapes=[dma((6,))],
    )(*[pltpu.with_memory_space_constraint(o, pltpu.VMEM) for o in outs])
    return tuple(finals)


def solution(mesh):
    tokens = P("batch", "seq", None)
    return jax.shard_map(
        on_device,
        mesh=mesh,
        in_specs=(tokens,) * 5 + (P(), P("batch", None)),
        out_specs=(tokens,) * 5 + (P("batch", None),),
        check_vma=False,
    )
```

time: 75.4 us -> 68.7 us (0.911)
  Pallas kernels: 74.7 us -> 68 us
    pallas_call x1, Pallas kernels: 73.4 us -> 66.7 us  [on_device(): pl.pallas_call(functools.partial(layer_kernel, token_total), out_shape=[v...]
where the time goes in v5:
time: 68.7 us; the launch traced here: 68.6 us
  Pallas kernels  68 us (99%)
    pallas_call x1, Pallas kernels, on_device(): pl.pallas_call(functools.partial(layer_kernel, token_total), out_shape=[v...  66.7 us

profile of v5, /device:TPU:1, one launch (start us, length us, event | category | flops | bytes accessed | tf_op | source)
XLA Modules:
  0.0 68.6 jit_solution(9390717291032406882)
XLA Ops:
  0.6 66.7 %shard_map.118 = (bf16[128,1024]{1,0:T(8,128)(2,1)S(1)}, bf16[128,1024]{1,0:T(8,128)(2,1)S(1)}, bf16[128,1024]{1,0:T(8,128)(2,1)S(1)}, bf16[128,1024]{1,0:T(8,12...) custom-call(s32[1,4]{1,0:T(1,128)} %len_hbm.1, bf16[1,128,1024]{2,1,0:T(8,128)(2,1)} %q_hbm.1, ...), custom_call_target="tpu_custom_call" | custom-call | tf_op jit(solution)/shard_map/pallas_call | solution.py:382
  67.3 1.3 %shard_map.119 = (bf16[1,128,1024]{2,1,0:T(8,128)(2,1)}, bf16[1,128,1024]{2,1,0:T(8,128)(2,1)}, bf16[1,128,1024]{2,1,0:T(8,128)(2,1)}, bf16[1,128,1024]{2,1,0:T(...) custom-call(bf16[128,1024]{1,0:T(8,128)(2,1)S(1)} %get-tuple-element.12.refs_0_, ...), custom_call_target="tpu_custom_call" | custom-call | tf_op jit(solution)/shard_map/pallas_call | solution.py:402

commit v6 on v5

--- a/solution.py
+++ b/solution.py
@@ -120,6 +120,10 @@
     def og_pass(c):
         block = og8.at[og_slot(3), og_rows(c)]
         return remote(block, block, ss_og, rs_og.at[4 + c], xs[2])
+
+    def og_pass_again(c):
+        block = og8.at[og_slot(2), og_rows(c)]
+        return remote(block, block, ss_og, rs_og.at[8], xs[2])
 
     def og_relay(d, c):
         block = og8.at[og_slot(d), og_rows(c)]
@@ -164,6 +168,9 @@
                 for which in range(2):
                     kv_relay(2 * c + i, which).start()
 
+        og_send(3, c).wait_recv()
+        og_pass(c).start()
+        og_relay(3, c).start()
         arrived(pair, rs_kv.at[1, c])
         for i in range(2):
             h = 2 * c + i
@@ -174,19 +181,16 @@
             att[h] = a
             slope[h] = jnp.where(ok, g * (1.0 + s * (1.0 - g)) * scale, 0.0)
             mixed[:, lanes(h)] = dot(a, vwin[h])
-        og_send(3, c).wait_recv()
-        og_pass(c).start()
-        og_relay(3, c).start()
-
-        @pl.when(c >= 1)
-        def _():
-            og_pass(c - 1).wait_recv()
-            og_relay(2, c - 1).start()
 
         @pl.when(c >= 2)
         def _():
-            og_send(1, 2 * c - 4).start()
-            og_send(1, 2 * c - 3).start()
+            og_pass(c - 2).wait_recv()
+            og_pass_again(c - 2).start()
+            og_relay(2, c - 2).start()
+
+        @pl.when(c >= 2)
+        def _():
+            og_send(1, c).start()
 
         return carry
 
@@ -219,8 +223,8 @@
     for r in (4, 3, 5, 2, 6, 7, 1):
         h_send(r).start()
     htr[me] = ht[me]
-    og_pass(3).wait_recv()
-    og_relay(2, 3).start()
+    og_pass(2).wait_recv()
+    og_relay(2, 2).start()
 
     def norm_back(i, carry):
         rows = pl.ds(pl.multiple_of(i * 16, 16), 16)
@@ -252,6 +256,8 @@
         return carry
 
     lax.fori_loop(0, HEADS, backward, 0)
+    og_pass(3).wait_recv()
+    og_relay(2, 3).start()
     arrived(og8.at[0], rs_og.at[8])
     block = og8.at[og_slot(1)]
     remote(block, block, ss_og, rs_og.at[9], partner).start()
@@ -302,15 +308,6 @@
         def _():
             z_send(d).start()
 
-    arrived(rg.at[1], rs_g.at[4])
-
-    def grads(h, carry):
-        total = go[h] + rg[1, h].astype(f32)
-        gk_ref[:, lanes(h)] = total[0].astype(bf16)
-        gv_ref[:, lanes(h)] = total[1].astype(bf16)
-        return carry
-
-    lax.fori_loop(0, HEADS, grads, 0)
 
     @pl.when(z < OWNERS)
     def _():
@@ -321,6 +318,16 @@
         ag[z] = t.astype(bf16)
         for d in far_first:
             a_send(d).start()
+
+    arrived(rg.at[1], rs_g.at[4])
+
+    def grads(h, carry):
+        total = go[h] + rg[1, h].astype(f32)
+        gk_ref[:, lanes(h)] = total[0].astype(bf16)
+        gv_ref[:, lanes(h)] = total[1].astype(bf16)
+        return carry
+
+    lax.fori_loop(0, HEADS, grads, 0)
 
     def f_send(r, p):
         return remote(ag.at[p], finr.at[me, p], ss_f, rs_f, slab_peer(r)[1])

time: 68.7 us -> 66.3 us (0.965)
  Pallas kernels: 68 us -> 65.5 us
    pallas_call x1, Pallas kernels: 66.7 us -> 64.2 us  [on_device(): pl.pallas_call(functools.partial(layer_kernel, token_total), out_shape=[v...]
where the time goes in v6:
time: 66.3 us; the launch traced here: 66.2 us
  Pallas kernels  65.5 us (99%)
    pallas_call x1, Pallas kernels, on_device(): pl.pallas_call(functools.partial(layer_kernel, token_total), out_shape=[v...  64.2 us

profile of v6, /device:TPU:1, one launch (start us, length us, event | category | flops | bytes accessed | tf_op | source)
XLA Modules:
  0.0 66.2 jit_solution(9304379429536423261)
XLA Ops:
  0.6 64.2 %shard_map.118 = (bf16[128,1024]{1,0:T(8,128)(2,1)S(1)}, bf16[128,1024]{1,0:T(8,128)(2,1)S(1)}, bf16[128,1024]{1,0:T(8,128)(2,1)S(1)}, bf16[128,1024]{1,0:T(8,12...) custom-call(s32[1,4]{1,0:T(1,128)} %len_hbm.1, bf16[1,128,1024]{2,1,0:T(8,128)(2,1)} %q_hbm.1, ...), custom_call_target="tpu_custom_call" | custom-call | tf_op jit(solution)/shard_map/pallas_call | solution.py:389
  64.9 1.3 %shard_map.119 = (bf16[1,128,1024]{2,1,0:T(8,128)(2,1)}, bf16[1,128,1024]{2,1,0:T(8,128)(2,1)}, bf16[1,128,1024]{2,1,0:T(8,128)(2,1)}, bf16[1,128,1024]{2,1,0:T(...) custom-call(bf16[128,1024]{1,0:T(8,128)(2,1)S(1)} %get-tuple-element.12.refs_0_, ...), custom_call_target="tpu_custom_call" | custom-call | tf_op jit(solution)/shard_map/pallas_call | solution.py:409

commit v7 on v6

--- a/solution.py
+++ b/solution.py
@@ -241,30 +241,10 @@
     def grad_send(b, h):
         return remote(pg.at[b, h], rg.at[b, h], ss_g.at[b], rs_g.at[4 if b else h // 2], ring(-2) if b else partner)
 
-    def backward(h, carry):
-        gm = gmix[:, lanes(h)]
-        da = dot(gm, vwin[h], LAST)
-        ds = (da * slope[h]).astype(bf16)
-        gq_ref[:, lanes(h)] = dot(ds, kwin[h]).astype(bf16)
-        gk = dot(ds, q[:, lanes(h)], FIRST)
-        gv = dot(att[h], gm, FIRST)
-        for which, val in enumerate((gk, gv)):
-            pg[0, h, which] = val[128:256].astype(bf16)
-            far[h, which] = val[0:128]
-            go[h, which] = val[256:384]
-        grad_send(0, h).start()
-        return carry
-
-    lax.fori_loop(0, HEADS, backward, 0)
-    og_pass(3).wait_recv()
-    og_relay(2, 3).start()
-    arrived(og8.at[0], rs_og.at[8])
-    block = og8.at[og_slot(1)]
-    remote(block, block, ss_og, rs_og.at[9], partner).start()
     low = (k == 0).astype(f32)
     high = (k == 1).astype(f32)
 
-    def combine(c, carry):
+    def combine(c):
         arrived(pair, rs_g.at[c])
         for i in range(2):
             h = 2 * c + i
@@ -272,9 +252,35 @@
             pg[1, h] = (far[h] + got * high).astype(bf16)
             go[h] = go[h] + got * low
             grad_send(1, h).start()
+
+    def backward(c, carry):
+        for i in range(2):
+            h = 2 * c + i
+            gm = gmix[:, lanes(h)]
+            da = dot(gm, vwin[h], LAST)
+            ds = (da * slope[h]).astype(bf16)
+            gq_ref[:, lanes(h)] = dot(ds, kwin[h]).astype(bf16)
+            gk = dot(ds, q[:, lanes(h)], FIRST)
+            gv = dot(att[h], gm, FIRST)
+            for which, val in enumerate((gk, gv)):
+                pg[0, h, which] = val[128:256].astype(bf16)
+                far[h, which] = val[0:128]
+                go[h, which] = val[256:384]
+            grad_send(0, h).start()
+
+        @pl.when(c >= 1)
+        def _():
+            combine(c - 1)
+
         return carry
 
-    lax.fori_loop(0, 4, combine, 0)
+    lax.fori_loop(0, 4, backward, 0)
+    og_pass(3).wait_recv()
+    og_relay(2, 3).start()
+    arrived(og8.at[0], rs_og.at[8])
+    block = og8.at[og_slot(1)]
+    remote(block, block, ss_og, rs_og.at[9], partner).start()
+    combine(3)
 
     arrived(og8.at[pl.ds(0, 4)], rs_og.at[9])
     arrived(ht.at[pl.ds(0, 7)], rs_h)

time: 66.3 us -> 67.2 us (1.014)
  Pallas kernels: 65.5 us -> 66.3 us
    pallas_call x1, Pallas kernels: 64.2 us -> 65 us  [on_device(): pl.pallas_call(functools.partial(layer_kernel, token_total), out_shape=[v...]
where the time goes in v7:
time: 67.2 us; the launch traced here: 67 us
  Pallas kernels  66.3 us (99%)
    pallas_call x1, Pallas kernels, on_device(): pl.pallas_call(functools.partial(layer_kernel, token_total), out_shape=[v...  65 us

profile of v7, /device:TPU:1, one launch (start us, length us, event | category | flops | bytes accessed | tf_op | source)
XLA Modules:
  0.0 67.0 jit_solution(2783195551291261561)
XLA Ops:
  0.6 65.0 %shard_map.118 = (bf16[128,1024]{1,0:T(8,128)(2,1)S(1)}, bf16[128,1024]{1,0:T(8,128)(2,1)S(1)}, bf16[128,1024]{1,0:T(8,128)(2,1)S(1)}, bf16[128,1024]{1,0:T(8,12...) custom-call(s32[1,4]{1,0:T(1,128)} %len_hbm.1, bf16[1,128,1024]{2,1,0:T(8,128)(2,1)} %q_hbm.1, ...), custom_call_target="tpu_custom_call" | custom-call | tf_op jit(solution)/shard_map/pallas_call | solution.py:395
  65.7 1.3 %shard_map.119 = (bf16[1,128,1024]{2,1,0:T(8,128)(2,1)}, bf16[1,128,1024]{2,1,0:T(8,128)(2,1)}, bf16[1,128,1024]{2,1,0:T(8,128)(2,1)}, bf16[1,128,1024]{2,1,0:T(...) custom-call(bf16[128,1024]{1,0:T(8,128)(2,1)S(1)} %get-tuple-element.12.refs_0_, ...), custom_call_target="tpu_custom_call" | custom-call | tf_op jit(solution)/shard_map/pallas_call | solution.py:415
